TPU v7x, 1024 devices: a whole 4x4x32 slice. The times are simulated.
1024 devices in a mesh: gx: 8 (over z_hi, x), gy: 16 (over z_lo), gz: 8 (over y, core).
Axes of the slice: x: 4, y: 4, z: 32 (z_hi: 2, z_lo: 16; z = z_hi * 16 + z_lo), core: 2. Of those that a mesh axis runs over, the one named last changes fastest.
Arguments:
- right_side: float32 [64, 256, 1024], P('gx', 'gy', 'gz'), may hold values from -6 to 6
- coefficient: float32 [64, 256, 1024], P('gx', 'gy', 'gz'), may hold values from 0.25 to 4
Outputs:
- solution: float32 [64, 256, 1024], P('gx', 'gy', 'gz')
- residual: float32 [64, 256, 1024], P('gx', 'gy', 'gz')
All inputs are finite; a program needn't handle non-finite values.
Results may differ from a plain program's by a relative error of at most 0.0003.
Values sent between devices are 32-bit elements; how exact they have to be, the bound alone decides.
A program may use at most 32 MiB of HBM per device.

v0:
```python
import jax
import jax.numpy as jnp
from jax import lax
from jax.sharding import PartitionSpec as P

LEVELS = 3
DEGREE = 4


cheb_low = 0.3
cheb_high = 2.0


def extended(block, sides, width):
    for axis, dim in sides:
        count = lax.axis_size(axis)
        forward = [(i, i + 1) for i in range(count - 1)]
        backward = [(target, source) for source, target in forward]
        low = lax.ppermute(
            lax.slice_in_dim(block, block.shape[dim] - width, None, axis=dim), axis, forward
        )
        high = lax.ppermute(lax.slice_in_dim(block, 0, width, axis=dim), axis, backward)
        block = jnp.concatenate([low, block, high], axis=dim)
    return block


def face_terms(padded):
    face_x = 0.5 * (padded[1:, 1:-1, 1:-1] + padded[:-1, 1:-1, 1:-1])
    face_y = 0.5 * (padded[1:-1, 1:, 1:-1] + padded[1:-1, :-1, 1:-1])
    face_z = 0.5 * (padded[1:-1, 1:-1, 1:] + padded[1:-1, 1:-1, :-1])
    diagonal = (
        face_x[1:]
        + face_x[:-1]
        + face_y[:, 1:]
        + face_y[:, :-1]
        + face_z[:, :, 1:]
        + face_z[:, :, :-1]
    )
    return (face_x, face_y, face_z, diagonal)


def apply_padded(padded, face_set, factor):
    face_x, face_y, face_z, diagonal = face_set
    flux_x = face_x * (padded[1:, 1:-1, 1:-1] - padded[:-1, 1:-1, 1:-1])
    flux_y = face_y * (padded[1:-1, 1:, 1:-1] - padded[1:-1, :-1, 1:-1])
    flux_z = face_z * (padded[1:-1, 1:-1, 1:] - padded[1:-1, 1:-1, :-1])
    result = (
        flux_x[:-1]
        - flux_x[1:]
        + (flux_y[:, :-1] - flux_y[:, 1:])
        + (flux_z[:, :, :-1] - flux_z[:, :, 1:])
    )
    return factor * result


def fine_halo(values):
    return extended(values, (("gx", 0), ("gy", 1), ("gz", 2)), 1)


def spread_halo(values):
    return extended(values, (("gx", 0), ("gy", 1), ("gz", 2)), 1)


def restrict(values):
    size_x, size_y, size_z = values.shape
    blocks = values.reshape(size_x // 2, 2, size_y // 2, 2, size_z // 2, 2)
    return jnp.mean(blocks, axis=(1, 3, 5))


def prolong(values):
    size_x, size_y, size_z = values.shape
    spread = jnp.broadcast_to(values[:, None, :, None, :, None], (size_x, 2, size_y, 2, size_z, 2))
    return spread.reshape(2 * size_x, 2 * size_y, 2 * size_z)


def smooth(right, initial, face_set, factor, padder):
    diagonal = face_set[3]
    centre = 0.5 * (cheb_high + cheb_low)
    half_width = 0.5 * (cheb_high - cheb_low)
    sigma_val = centre / half_width
    rho_now = 1.0 / sigma_val
    if initial is None:
        iterate = jnp.zeros_like(right)
        leftover = right
    else:
        iterate = initial
        leftover = right - apply_padded(padder(initial), face_set, factor)
    update = leftover / (factor * diagonal) / centre
    iterate = iterate + update
    for sweep_no in range(DEGREE - 1):
        leftover = right - apply_padded(padder(iterate), face_set, factor)
        rho_next = 1.0 / (2.0 * sigma_val - rho_now)
        update = rho_next * rho_now * update + 2.0 * rho_next / half_width * (
            leftover / (factor * diagonal)
        )
        iterate = iterate + update
        rho_now = rho_next
    return iterate


def per_device(right_side, coefficient):
    fine_set = face_terms(fine_halo(coefficient))
    iterate = smooth(right_side, None, fine_set, 1.0, fine_halo)
    leftover = right_side - apply_padded(fine_halo(iterate), fine_set, 1.0)
    coarse_right = restrict(leftover)
    coarse_coef = restrict(coefficient)
    rights = [coarse_right]
    face_sets = []
    iterates = []
    for level_no in range(1, LEVELS):
        factor = 0.25**level_no
        face_set = face_terms(spread_halo(coarse_coef))
        face_sets.append(face_set)
        current = smooth(rights[-1], None, face_set, factor, spread_halo)
        iterates.append(current)
        if level_no < LEVELS - 1:
            remains = rights[-1] - apply_padded(spread_halo(current), face_set, factor)
            rights.append(restrict(remains))
            coarse_coef = restrict(coarse_coef)
    level_no = 1
    slot_no = level_no - 1
    iterates[slot_no] = smooth(
        rights[slot_no],
        iterates[slot_no] + prolong(iterates[slot_no + 1]),
        face_sets[slot_no],
        0.25**level_no,
        spread_halo,
    )
    correction = iterates[0]
    start = iterate + prolong(correction)
    solution = smooth(right_side, start, fine_set, 1.0, fine_halo)
    residual = right_side - apply_padded(fine_halo(solution), fine_set, 1.0)
    return (solution, residual)


def solution(mesh):
    in_specs = (P("gx", "gy", "gz"), P("gx", "gy", "gz"))
    out_specs = (P("gx", "gy", "gz"), P("gx", "gy", "gz"))
    return jax.shard_map(
        per_device, mesh=mesh, in_specs=in_specs, out_specs=out_specs, check_vma=False
    )
```

profile of v0, /device:TPU:14, one launch (start us, length us, event | category | flops | bytes accessed | tf_op | source)
XLA Modules:
  0.0 1044.7 jit_solution(9801258370503566079)
XLA Ops:
  4.1 28.2 %collective-permute-start.1 = (f32[1,16,128]{2,1,0:T(8,128)S(1)}, f32[1,16,128]{2,1,0:T(8,128)S(1)}, u32[]{:S(2)}, u32[]{:S(2)}) collective-permute-start(f32[1,16,128]{2,1,0:T(8,128)S(1)} %get-tuple-element.91), channel_id=1, source_target_pairs={{0,128},{128,256},{256,384},{384,512},{512,640},{640,768},{768,896... | collective-permute-start | bytes 24584 | tf_op jit(solution)/shard_map/ppermute | solution.py:19
  32.3 6.3 reshape.26
  47.8 24.4 %collective-permute-start.31 = (f32[1,8,64]{2,1,0:T(8,128)S(1)}, f32[1,8,64]{2,1,0:T(8,128)S(1)}, u32[]{:S(2)}, u32[]{:S(2)}) collective-permute-start(f32[1,8,64]{2,1,0:T(8,128)S(1)} %get-tuple-element.152), channel_id=1, source_target_pairs={{0,128},{128,256},{256,384},{384,512},{512,640},{640,768},{768,896... | collective-permute-start | bytes 6152 | tf_op jit(solution)/shard_map/ppermute | solution.py:19
  78.3 19.7 %collective-permute-done.30 = f32[1,8,64]{2,1,0:T(8,128)S(1)} collective-permute-done((f32[1,8,64]{2,1,0:T(8,128)S(1)}, f32[1,8,64]{2,1,0:T(8,128)S(1)}, u32[]{:S(2)}, u32[]{:S(2)}) %collective-permute-start.30) | collective-permute-done | bytes 2080 | tf_op jit(solution)/shard_map/ppermute | solution.py:22
  118.1 6.3 collective-permute-start.7
  126.3 24.1 %collective-permute-done.6 = f32[1,16,128]{2,1,0:T(8,128)S(1)} collective-permute-done((f32[1,16,128]{2,1,0:T(8,128)S(1)}, f32[1,16,128]{2,1,0:T(8,128)S(1)}, u32[]{:S(2)}, u32[]{:S(2)}) %collective-permute-start.6) | collective-permute-done | bytes 8224 | tf_op jit(solution)/shard_map/ppermute | solution.py:22
  154.8 4.2 collective-permute-done.8
  175.5 20.0 %collective-permute-done.12 = f32[1,16,128]{2,1,0:T(8,128)S(1)} collective-permute-done((f32[1,16,128]{2,1,0:T(8,128)S(1)}, f32[1,16,128]{2,1,0:T(8,128)S(1)}, u32[]{:S(2)}, u32[]{:S(2)}) %collective-permute-start.12) | collective-permute-done | bytes 8224 | tf_op jit(solution)/shard_map/ppermute | solution.py:22
  219.4 22.4 %collective-permute-done.18 = f32[1,16,128]{2,1,0:T(8,128)S(1)} collective-permute-done((f32[1,16,128]{2,1,0:T(8,128)S(1)}, f32[1,16,128]{2,1,0:T(8,128)S(1)}, u32[]{:S(2)}, u32[]{:S(2)}) %collective-permute-start.18) | collective-permute-done | bytes 8224 | tf_op jit(solution)/shard_map/ppermute | solution.py:22
  265.7 21.9 %collective-permute-done.24 = f32[1,16,128]{2,1,0:T(8,128)S(1)} collective-permute-done((f32[1,16,128]{2,1,0:T(8,128)S(1)}, f32[1,16,128]{2,1,0:T(8,128)S(1)}, u32[]{:S(2)}, u32[]{:S(2)}) %collective-permute-start.24) | collective-permute-done | bytes 8224 | tf_op jit(solution)/shard_map/ppermute | solution.py:22
  287.6 4.4 collective-permute-start.27
  306.1 5.6 reshape.25
  320.2 22.0 %collective-permute-done.36 = f32[1,8,64]{2,1,0:T(8,128)S(1)} collective-permute-done((f32[1,8,64]{2,1,0:T(8,128)S(1)}, f32[1,8,64]{2,1,0:T(8,128)S(1)}, u32[]{:S(2)}, u32[]{:S(2)}) %collective-permute-start.36) | collective-permute-done | bytes 2080 | tf_op jit(solution)/shard_map/ppermute | solution.py:22
  369.4 17.6 %collective-permute-done.42 = f32[1,8,64]{2,1,0:T(8,128)S(1)} collective-permute-done((f32[1,8,64]{2,1,0:T(8,128)S(1)}, f32[1,8,64]{2,1,0:T(8,128)S(1)}, u32[]{:S(2)}, u32[]{:S(2)}) %collective-permute-start.42) | collective-permute-done | bytes 2080 | tf_op jit(solution)/shard_map/ppermute | solution.py:22
  387.1 4.8 collective-permute-start.45
  404.9 4.9 collective-permute-start.49
  411.8 24.0 %collective-permute-done.48 = f32[1,8,64]{2,1,0:T(8,128)S(1)} collective-permute-done((f32[1,8,64]{2,1,0:T(8,128)S(1)}, f32[1,8,64]{2,1,0:T(8,128)S(1)}, u32[]{:S(2)}, u32[]{:S(2)}) %collective-permute-start.48) | collective-permute-done | bytes 2080 | tf_op jit(solution)/shard_map/ppermute | solution.py:22
  435.8 5.1 collective-permute-start.51
  460.0 21.9 %collective-permute-done.54 = f32[1,8,64]{2,1,0:T(8,128)S(1)} collective-permute-done((f32[1,8,64]{2,1,0:T(8,128)S(1)}, f32[1,8,64]{2,1,0:T(8,128)S(1)}, u32[]{:S(2)}, u32[]{:S(2)}) %collective-permute-start.54) | collective-permute-done | bytes 2080 | tf_op jit(solution)/shard_map/ppermute | solution.py:22
  505.5 22.0 %collective-permute-done.66 = f32[1,4,32]{2,1,0:T(4,128)S(1)} collective-permute-done((f32[1,4,32]{2,1,0:T(4,128)S(1)}, f32[1,4,32]{2,1,0:T(4,128)S(1)}, u32[]{:S(2)}, u32[]{:S(2)}) %collective-permute-start.66) | collective-permute-done | bytes 544 | tf_op jit(solution)/shard_map/ppermute | solution.py:22
  527.5 4.4 collective-permute-start.69
  550.5 22.0 %collective-permute-done.72 = f32[1,4,32]{2,1,0:T(4,128)S(1)} collective-permute-done((f32[1,4,32]{2,1,0:T(4,128)S(1)}, f32[1,4,32]{2,1,0:T(4,128)S(1)}, u32[]{:S(2)}, u32[]{:S(2)}) %collective-permute-start.72) | collective-permute-done | bytes 544 | tf_op jit(solution)/shard_map/ppermute | solution.py:22
  595.2 22.0 %collective-permute-done.78 = f32[1,4,32]{2,1,0:T(4,128)S(1)} collective-permute-done((f32[1,4,32]{2,1,0:T(4,128)S(1)}, f32[1,4,32]{2,1,0:T(4,128)S(1)}, u32[]{:S(2)}, u32[]{:S(2)}) %collective-permute-start.78) | collective-permute-done | bytes 544 | tf_op jit(solution)/shard_map/ppermute | solution.py:22
  640.1 22.0 %collective-permute-done.84 = f32[1,8,64]{2,1,0:T(8,128)S(1)} collective-permute-done((f32[1,8,64]{2,1,0:T(8,128)S(1)}, f32[1,8,64]{2,1,0:T(8,128)S(1)}, u32[]{:S(2)}, u32[]{:S(2)}) %collective-permute-start.84) | collective-permute-done | bytes 2080 | tf_op jit(solution)/shard_map/ppermute | solution.py:22
  684.9 22.0 %collective-permute-done.90 = f32[1,8,64]{2,1,0:T(8,128)S(1)} collective-permute-done((f32[1,8,64]{2,1,0:T(8,128)S(1)}, f32[1,8,64]{2,1,0:T(8,128)S(1)}, u32[]{:S(2)}, u32[]{:S(2)}) %collective-permute-start.90) | collective-permute-done | bytes 2080 | tf_op jit(solution)/shard_map/ppermute | solution.py:22
  729.2 22.0 %collective-permute-done.96 = f32[1,8,64]{2,1,0:T(8,128)S(1)} collective-permute-done((f32[1,8,64]{2,1,0:T(8,128)S(1)}, f32[1,8,64]{2,1,0:T(8,128)S(1)}, u32[]{:S(2)}, u32[]{:S(2)}) %collective-permute-start.96) | collective-permute-done | bytes 2080 | tf_op jit(solution)/shard_map/ppermute | solution.py:22
  773.4 22.0 %collective-permute-done.102 = f32[1,8,64]{2,1,0:T(8,128)S(1)} collective-permute-done((f32[1,8,64]{2,1,0:T(8,128)S(1)}, f32[1,8,64]{2,1,0:T(8,128)S(1)}, u32[]{:S(2)}, u32[]{:S(2)}) %collective-permute-start.102) | collective-permute-done | bytes 2080 | tf_op jit(solution)/shard_map/ppermute | solution.py:22
  824.1 22.0 %collective-permute-done.108 = f32[1,16,128]{2,1,0:T(8,128)S(1)} collective-permute-done((f32[1,16,128]{2,1,0:T(8,128)S(1)}, f32[1,16,128]{2,1,0:T(8,128)S(1)}, u32[]{:S(2)}, u32[]{:S(2)}) %collective-permute-start.108) | collective-permute-done | bytes 8224 | tf_op jit(solution)/shard_map/ppermute | solution.py:22
  869.3 22.0 %collective-permute-done.114 = f32[1,16,128]{2,1,0:T(8,128)S(1)} collective-permute-done((f32[1,16,128]{2,1,0:T(8,128)S(1)}, f32[1,16,128]{2,1,0:T(8,128)S(1)}, u32[]{:S(2)}, u32[]{:S(2)}) %collective-permute-start.114) | collective-permute-done | bytes 8224 | tf_op jit(solution)/shard_map/ppermute | solution.py:22
  914.4 22.0 %collective-permute-done.120 = f32[1,16,128]{2,1,0:T(8,128)S(1)} collective-permute-done((f32[1,16,128]{2,1,0:T(8,128)S(1)}, f32[1,16,128]{2,1,0:T(8,128)S(1)}, u32[]{:S(2)}, u32[]{:S(2)}) %collective-permute-start.120) | collective-permute-done | bytes 8224 | tf_op jit(solution)/shard_map/ppermute | solution.py:22
  959.7 22.0 %collective-permute-done.126 = f32[1,16,128]{2,1,0:T(8,128)S(1)} collective-permute-done((f32[1,16,128]{2,1,0:T(8,128)S(1)}, f32[1,16,128]{2,1,0:T(8,128)S(1)}, u32[]{:S(2)}, u32[]{:S(2)}) %collective-permute-start.126) | collective-permute-done | bytes 8224 | tf_op jit(solution)/shard_map/ppermute | solution.py:22
  1004.8 22.0 %collective-permute-done.132 = f32[1,16,128]{2,1,0:T(8,128)S(1)} collective-permute-done((f32[1,16,128]{2,1,0:T(8,128)S(1)}, f32[1,16,128]{2,1,0:T(8,128)S(1)}, u32[]{:S(2)}, u32[]{:S(2)}) %collective-permute-start.132) | collective-permute-done | bytes 8224 | tf_op jit(solution)/shard_map/ppermute | solution.py:22
  (453 shorter events, 485.2 us)
Async XLA Ops:
  1.3 99.7 %collective-permute-start = (f32[1,16,128]{2,1,0:T(8,128)S(1)}, f32[1,16,128]{2,1,0:T(8,128)S(1)}, u32[]{:S(2)}, u32[]{:S(2)}) collective-permute-start(f32[1,16,128]{2,1,0:T(8,128)S(1)} %get-tuple-element.90), channel_id=1, source_target_pairs={{128,0},{256,128},{384,256},{512,384},{640,512},{768,640},{896,768... | collective-permute-start | bytes 24584 | tf_op jit(solution)/shard_map/ppermute | solution.py:22
  4.1 96.9 %collective-permute-start.1 = (f32[1,16,128]{2,1,0:T(8,128)S(1)}, f32[1,16,128]{2,1,0:T(8,128)S(1)}, u32[]{:S(2)}, u32[]{:S(2)}) collective-permute-start(f32[1,16,128]{2,1,0:T(8,128)S(1)} %get-tuple-element.91), channel_id=1, source_target_pairs={{0,128},{128,256},{256,384},{384,512},{512,640},{640,768},{768,896... | collective-permute-start | bytes 24584 | tf_op jit(solution)/shard_map/ppermute | solution.py:19
  41.9 30.2 %collective-permute-start.61 = (f32[1,4,32]{2,1,0:T(4,128)S(1)}, f32[1,4,32]{2,1,0:T(4,128)S(1)}, u32[]{:S(2)}, u32[]{:S(2)}) collective-permute-start(f32[1,4,32]{2,1,0:T(4,128)S(1)} %get-tuple-element.168), channel_id=1, source_target_pairs={{0,128},{128,256},{256,384},{384,512},{512,640},{640,768},{768,896... | collective-permute-start | bytes 1544 | tf_op jit(solution)/shard_map/ppermute | solution.py:19
  45.8 28.2 %collective-permute-start.60 = (f32[1,4,32]{2,1,0:T(4,128)S(1)}, f32[1,4,32]{2,1,0:T(4,128)S(1)}, u32[]{:S(2)}, u32[]{:S(2)}) collective-permute-start(f32[1,4,32]{2,1,0:T(4,128)S(1)} %get-tuple-element.169), channel_id=1, source_target_pairs={{128,0},{256,128},{384,256},{512,384},{640,512},{768,640},{896,768... | collective-permute-start | bytes 1544 | tf_op jit(solution)/shard_map/ppermute | solution.py:22
  47.8 29.3 %collective-permute-start.31 = (f32[1,8,64]{2,1,0:T(8,128)S(1)}, f32[1,8,64]{2,1,0:T(8,128)S(1)}, u32[]{:S(2)}, u32[]{:S(2)}) collective-permute-start(f32[1,8,64]{2,1,0:T(8,128)S(1)} %get-tuple-element.152), channel_id=1, source_target_pairs={{0,128},{128,256},{256,384},{384,512},{512,640},{640,768},{768,896... | collective-permute-start | bytes 6152 | tf_op jit(solution)/shard_map/ppermute | solution.py:19
  72.1 25.9 %collective-permute-start.30 = (f32[1,8,64]{2,1,0:T(8,128)S(1)}, f32[1,8,64]{2,1,0:T(8,128)S(1)}, u32[]{:S(2)}, u32[]{:S(2)}) collective-permute-start(f32[1,8,64]{2,1,0:T(8,128)S(1)} %get-tuple-element.153), channel_id=1, source_target_pairs={{128,0},{256,128},{384,256},{512,384},{640,512},{768,640},{896,768... | collective-permute-start | bytes 6152 | tf_op jit(solution)/shard_map/ppermute | solution.py:22
  74.1 246.0 %collective-permute-start.63 = (f32[4,1,32]{2,1,0:T(1,128)S(1)}, f32[4,1,32]{2,1,0:T(1,128)S(1)}, u32[]{:S(2)}, u32[]{:S(2)}) collective-permute-start(f32[4,1,32]{2,1,0:T(1,128)S(1)} %get-tuple-element.160), channel_id=1, source_target_pairs={{0,8},{8,16},{16,24},{24,32},{32,40},{40,48},{48,56},{56,64},{64,7... | collective-permute-start | bytes 1544 | tf_op jit(solution)/shard_map/ppermute | solution.py:19
  77.0 243.1 %collective-permute-start.62 = (f32[4,1,32]{2,1,0:T(1,128)S(1)}, f32[4,1,32]{2,1,0:T(1,128)S(1)}, u32[]{:S(2)}, u32[]{:S(2)}) collective-permute-start(f32[4,1,32]{2,1,0:T(1,128)S(1)} %get-tuple-element.161), channel_id=1, source_target_pairs={{8,0},{16,8},{24,16},{32,24},{40,32},{48,40},{56,48},{64,56},{72,6... | collective-permute-start | bytes 1544 | tf_op jit(solution)/shard_map/ppermute | solution.py:22
  98.1 26.3 %collective-permute-start.33 = (f32[6,1,64]{2,1,0:T(1,128)S(1)}, f32[6,1,64]{2,1,0:T(1,128)S(1)}, u32[]{:S(2)}, u32[]{:S(2)}) collective-permute-start(f32[6,1,64]{2,1,0:T(1,128)S(1)} %get-tuple-element.126), channel_id=1, source_target_pairs={{0,8},{8,16},{16,24},{24,32},{32,40},{40,48},{48,56},{56,64},{64,7... | collective-permute-start | bytes 4616 | tf_op jit(solution)/shard_map/ppermute | solution.py:19
  124.4 26.0 %collective-permute-start.6 = (f32[1,16,128]{2,1,0:T(8,128)S(1)}, f32[1,16,128]{2,1,0:T(8,128)S(1)}, u32[]{:S(2)}, u32[]{:S(2)}) collective-permute-start(f32[1,16,128]{2,1,0:T(8,128)S(1)} %get-tuple-element.89), channel_id=1, source_target_pairs={{128,0},{256,128},{384,256},{512,384},{640,512},{768,640},{896,768... | collective-permute-start | bytes 24584 | tf_op jit(solution)/shard_map/ppermute | solution.py:22
  169.5 26.0 %collective-permute-start.12 = (f32[1,16,128]{2,1,0:T(8,128)S(1)}, f32[1,16,128]{2,1,0:T(8,128)S(1)}, u32[]{:S(2)}, u32[]{:S(2)}) collective-permute-start(f32[1,16,128]{2,1,0:T(8,128)S(1)} %get-tuple-element.87), channel_id=1, source_target_pairs={{128,0},{256,128},{384,256},{512,384},{640,512},{768,640},{896,768... | collective-permute-start | bytes 24584 | tf_op jit(solution)/shard_map/ppermute | solution.py:22
  173.5 88.1 %collective-permute-start.34 = (f32[6,10,1]{2,1,0:T(8,128)S(1)}, f32[6,10,1]{2,1,0:T(8,128)S(1)}, u32[]{:S(2)}, u32[]{:S(2)}) collective-permute-start(f32[6,10,1]{2,1,0:T(8,128)S(1)} %get-tuple-element.108), channel_id=1, source_target_pairs={{1,0},{2,1},{3,2},{4,3},{5,4},{6,5},{7,6},{9,8},{10,9},{11,10},{12... | collective-permute-start | bytes 728 | tf_op jit(solution)/shard_map/ppermute | solution.py:22
  215.9 26.0 %collective-permute-start.18 = (f32[1,16,128]{2,1,0:T(8,128)S(1)}, f32[1,16,128]{2,1,0:T(8,128)S(1)}, u32[]{:S(2)}, u32[]{:S(2)}) collective-permute-start(f32[1,16,128]{2,1,0:T(8,128)S(1)} %get-tuple-element.85), channel_id=1, source_target_pairs={{128,0},{256,128},{384,256},{512,384},{640,512},{768,640},{896,768... | collective-permute-start | bytes 24584 | tf_op jit(solution)/shard_map/ppermute | solution.py:22
  261.6 26.0 %collective-permute-start.24 = (f32[1,16,128]{2,1,0:T(8,128)S(1)}, f32[1,16,128]{2,1,0:T(8,128)S(1)}, u32[]{:S(2)}, u32[]{:S(2)}) collective-permute-start(f32[1,16,128]{2,1,0:T(8,128)S(1)} %get-tuple-element.83), channel_id=1, source_target_pairs={{128,0},{256,128},{384,256},{512,384},{640,512},{768,640},{896,768... | collective-permute-start | bytes 24584 | tf_op jit(solution)/shard_map/ppermute | solution.py:22
  316.2 25.9 %collective-permute-start.36 = (f32[1,8,64]{2,1,0:T(8,128)S(1)}, f32[1,8,64]{2,1,0:T(8,128)S(1)}, u32[]{:S(2)}, u32[]{:S(2)}) collective-permute-start(f32[1,8,64]{2,1,0:T(8,128)S(1)} %get-tuple-element.151), channel_id=1, source_target_pairs={{128,0},{256,128},{384,256},{512,384},{640,512},{768,640},{896,768... | collective-permute-start | bytes 6152 | tf_op jit(solution)/shard_map/ppermute | solution.py:22
  361.1 25.9 %collective-permute-start.42 = (f32[1,8,64]{2,1,0:T(8,128)S(1)}, f32[1,8,64]{2,1,0:T(8,128)S(1)}, u32[]{:S(2)}, u32[]{:S(2)}) collective-permute-start(f32[1,8,64]{2,1,0:T(8,128)S(1)} %get-tuple-element.149), channel_id=1, source_target_pairs={{128,0},{256,128},{384,256},{512,384},{640,512},{768,640},{896,768... | collective-permute-start | bytes 6152 | tf_op jit(solution)/shard_map/ppermute | solution.py:22
  365.1 94.8 %collective-permute-start.64 = (f32[4,6,1]{2,1,0:T(8,128)S(1)}, f32[4,6,1]{2,1,0:T(8,128)S(1)}, u32[]{:S(2)}, u32[]{:S(2)}) collective-permute-start(f32[4,6,1]{2,1,0:T(8,128)S(1)} %get-tuple-element.142), channel_id=1, source_target_pairs={{1,0},{2,1},{3,2},{4,3},{5,4},{6,5},{7,6},{9,8},{10,9},{11,10},{12... | collective-permute-start | bytes 296 | tf_op jit(solution)/shard_map/ppermute | solution.py:22
  367.0 92.8 %collective-permute-start.65 = (f32[4,6,1]{2,1,0:T(8,128)S(1)}, f32[4,6,1]{2,1,0:T(8,128)S(1)}, u32[]{:S(2)}, u32[]{:S(2)}) collective-permute-start(f32[4,6,1]{2,1,0:T(8,128)S(1)} %get-tuple-element.143), channel_id=1, source_target_pairs={{0,1},{1,2},{2,3},{3,4},{4,5},{5,6},{6,7},{8,9},{9,10},{10,11},{11... | collective-permute-start | bytes 296 | tf_op jit(solution)/shard_map/ppermute | solution.py:19
  409.8 25.9 %collective-permute-start.48 = (f32[1,8,64]{2,1,0:T(8,128)S(1)}, f32[1,8,64]{2,1,0:T(8,128)S(1)}, u32[]{:S(2)}, u32[]{:S(2)}) collective-permute-start(f32[1,8,64]{2,1,0:T(8,128)S(1)} %get-tuple-element.147), channel_id=1, source_target_pairs={{128,0},{256,128},{384,256},{512,384},{640,512},{768,640},{896,768... | collective-permute-start | bytes 6152 | tf_op jit(solution)/shard_map/ppermute | solution.py:22
  455.9 25.9 %collective-permute-start.54 = (f32[1,8,64]{2,1,0:T(8,128)S(1)}, f32[1,8,64]{2,1,0:T(8,128)S(1)}, u32[]{:S(2)}, u32[]{:S(2)}) collective-permute-start(f32[1,8,64]{2,1,0:T(8,128)S(1)} %get-tuple-element.145), channel_id=1, source_target_pairs={{128,0},{256,128},{384,256},{512,384},{640,512},{768,640},{896,768... | collective-permute-start | bytes 6152 | tf_op jit(solution)/shard_map/ppermute | solution.py:22
  501.5 25.9 %collective-permute-start.66 = (f32[1,4,32]{2,1,0:T(4,128)S(1)}, f32[1,4,32]{2,1,0:T(4,128)S(1)}, u32[]{:S(2)}, u32[]{:S(2)}) collective-permute-start(f32[1,4,32]{2,1,0:T(4,128)S(1)} %get-tuple-element.167), channel_id=1, source_target_pairs={{128,0},{256,128},{384,256},{512,384},{640,512},{768,640},{896,768... | collective-permute-start | bytes 1544 | tf_op jit(solution)/shard_map/ppermute | solution.py:22
  546.6 25.9 %collective-permute-start.72 = (f32[1,4,32]{2,1,0:T(4,128)S(1)}, f32[1,4,32]{2,1,0:T(4,128)S(1)}, u32[]{:S(2)}, u32[]{:S(2)}) collective-permute-start(f32[1,4,32]{2,1,0:T(4,128)S(1)} %get-tuple-element.165), channel_id=1, source_target_pairs={{128,0},{256,128},{384,256},{512,384},{640,512},{768,640},{896,768... | collective-permute-start | bytes 1544 | tf_op jit(solution)/shard_map/ppermute | solution.py:22
  591.2 25.9 %collective-permute-start.78 = (f32[1,4,32]{2,1,0:T(4,128)S(1)}, f32[1,4,32]{2,1,0:T(4,128)S(1)}, u32[]{:S(2)}, u32[]{:S(2)}) collective-permute-start(f32[1,4,32]{2,1,0:T(4,128)S(1)} %get-tuple-element.163), channel_id=1, source_target_pairs={{128,0},{256,128},{384,256},{512,384},{640,512},{768,640},{896,768... | collective-permute-start | bytes 1544 | tf_op jit(solution)/shard_map/ppermute | solution.py:22
  636.2 25.9 %collective-permute-start.84 = (f32[1,8,64]{2,1,0:T(8,128)S(1)}, f32[1,8,64]{2,1,0:T(8,128)S(1)}, u32[]{:S(2)}, u32[]{:S(2)}) collective-permute-start(f32[1,8,64]{2,1,0:T(8,128)S(1)} %get-tuple-element.135), channel_id=1, source_target_pairs={{128,0},{256,128},{384,256},{512,384},{640,512},{768,640},{896,768... | collective-permute-start | bytes 6152 | tf_op jit(solution)/shard_map/ppermute | solution.py:22
  681.0 25.9 %collective-permute-start.90 = (f32[1,8,64]{2,1,0:T(8,128)S(1)}, f32[1,8,64]{2,1,0:T(8,128)S(1)}, u32[]{:S(2)}, u32[]{:S(2)}) collective-permute-start(f32[1,8,64]{2,1,0:T(8,128)S(1)} %get-tuple-element.133), channel_id=1, source_target_pairs={{128,0},{256,128},{384,256},{512,384},{640,512},{768,640},{896,768... | collective-permute-start | bytes 6152 | tf_op jit(solution)/shard_map/ppermute | solution.py:22
  725.3 25.9 %collective-permute-start.96 = (f32[1,8,64]{2,1,0:T(8,128)S(1)}, f32[1,8,64]{2,1,0:T(8,128)S(1)}, u32[]{:S(2)}, u32[]{:S(2)}) collective-permute-start(f32[1,8,64]{2,1,0:T(8,128)S(1)} %get-tuple-element.131), channel_id=1, source_target_pairs={{128,0},{256,128},{384,256},{512,384},{640,512},{768,640},{896,768... | collective-permute-start | bytes 6152 | tf_op jit(solution)/shard_map/ppermute | solution.py:22
  769.4 25.9 %collective-permute-start.102 = (f32[1,8,64]{2,1,0:T(8,128)S(1)}, f32[1,8,64]{2,1,0:T(8,128)S(1)}, u32[]{:S(2)}, u32[]{:S(2)}) collective-permute-start(f32[1,8,64]{2,1,0:T(8,128)S(1)} %get-tuple-element.129), channel_id=1, source_target_pairs={{128,0},{256,128},{384,256},{512,384},{640,512},{768,640},{896,768... | collective-permute-start | bytes 6152 | tf_op jit(solution)/shard_map/ppermute | solution.py:22
  820.2 26.0 %collective-permute-start.108 = (f32[1,16,128]{2,1,0:T(8,128)S(1)}, f32[1,16,128]{2,1,0:T(8,128)S(1)}, u32[]{:S(2)}, u32[]{:S(2)}) collective-permute-start(f32[1,16,128]{2,1,0:T(8,128)S(1)} %get-tuple-element.81), channel_id=1, source_target_pairs={{128,0},{256,128},{384,256},{512,384},{640,512},{768,640},{896,768... | collective-permute-start | bytes 24584 | tf_op jit(solution)/shard_map/ppermute | solution.py:22
  865.3 26.0 %collective-permute-start.114 = (f32[1,16,128]{2,1,0:T(8,128)S(1)}, f32[1,16,128]{2,1,0:T(8,128)S(1)}, u32[]{:S(2)}, u32[]{:S(2)}) collective-permute-start(f32[1,16,128]{2,1,0:T(8,128)S(1)} %get-tuple-element.79), channel_id=1, source_target_pairs={{128,0},{256,128},{384,256},{512,384},{640,512},{768,640},{896,768... | collective-permute-start | bytes 24584 | tf_op jit(solution)/shard_map/ppermute | solution.py:22
  910.4 26.0 %collective-permute-start.120 = (f32[1,16,128]{2,1,0:T(8,128)S(1)}, f32[1,16,128]{2,1,0:T(8,128)S(1)}, u32[]{:S(2)}, u32[]{:S(2)}) collective-permute-start(f32[1,16,128]{2,1,0:T(8,128)S(1)} %get-tuple-element.77), channel_id=1, source_target_pairs={{128,0},{256,128},{384,256},{512,384},{640,512},{768,640},{896,768... | collective-permute-start | bytes 24584 | tf_op jit(solution)/shard_map/ppermute | solution.py:22
  955.7 26.0 %collective-permute-start.126 = (f32[1,16,128]{2,1,0:T(8,128)S(1)}, f32[1,16,128]{2,1,0:T(8,128)S(1)}, u32[]{:S(2)}, u32[]{:S(2)}) collective-permute-start(f32[1,16,128]{2,1,0:T(8,128)S(1)} %get-tuple-element.75), channel_id=1, source_target_pairs={{128,0},{256,128},{384,256},{512,384},{640,512},{768,640},{896,768... | collective-permute-start | bytes 24584 | tf_op jit(solution)/shard_map/ppermute | solution.py:22
  1000.9 26.0 %collective-permute-start.132 = (f32[1,16,128]{2,1,0:T(8,128)S(1)}, f32[1,16,128]{2,1,0:T(8,128)S(1)}, u32[]{:S(2)}, u32[]{:S(2)}) collective-permute-start(f32[1,16,128]{2,1,0:T(8,128)S(1)} %get-tuple-element.73), channel_id=1, source_target_pairs={{128,0},{256,128},{384,256},{512,384},{640,512},{768,640},{896,768... | collective-permute-start | bytes 24584 | tf_op jit(solution)/shard_map/ppermute | solution.py:22
  (109 other events, 805.0 us)
where the time goes:
time: 1050 us; the launch traced here: 1040 us
  waiting for transfers between devices  609 us (58%)
  starting transfers between devices  397 us (38%)
  local copies, waits for them, and re-layouts  22.7 us (2%)
  other arithmetic  12.6 us (1%)
    ppermute x69, waiting for transfers between devices, extended(): lax.ppermute(lax.slice_in_dim(block, 0, width, axis=dim), axis, backward)  545 us
    ppermute x69, starting transfers between devices, extended(): lax.ppermute(lax.slice_in_dim(block, block.shape[dim] - width, None, axis...  243 us
    ppermute x69, starting transfers between devices, extended(): lax.ppermute(lax.slice_in_dim(block, 0, width, axis=dim), axis, backward)  154 us
    ppermute x69, waiting for transfers between devices, extended(): lax.ppermute(lax.slice_in_dim(block, block.shape[dim] - width, None, axis...  63.8 us
  transfers between devices with their start and end apart: 138, of which 62 were waited for; matrix products, arithmetic and copies ran while one was open for 2% of the time, Pallas kernels for 0%

commit v1 on v0

v1 whole, which is shorter than its diff:
```python
import functools

import jax
import jax.numpy as jnp
from jax import lax
from jax.experimental import pallas as pl
from jax.experimental.pallas import tpu as pltpu
from jax.sharding import PartitionSpec as P

DEGREE = 4
cheb_low = 0.3
cheb_high = 2.0
CENTRE = 0.5 * (cheb_high + cheb_low)
HALF = 0.5 * (cheb_high - cheb_low)
SIGMA = CENTRE / HALF
MESH = pl.DeviceIdType.MESH
CHUNKS = 2


def kernel(sizes, right_ref, coef_ref, sol_ref, res_ref, *scratch):
    (x0, x1, x2, g0, g1, g2, u0, u1, u2, b0, b1, b2, d0, d1, d2, hy, sy, hz, sz,
     relay_b, relay_k, send_sem, recv_sem, relay_send, relay_recv) = scratch
    xs, gs, us, bs, ds = (x0, x1, x2), (g0, g1, g2), (u0, u1, u2), (b0, b1, b2), (d0, d1, d2)
    size_gx, size_gy, size_gz = sizes
    half = size_gx // 2
    gx, gy, gz = lax.axis_index("gx"), lax.axis_index("gy"), lax.axis_index("gz")
    own = gx // half
    x = gx % half
    stages = relay_b.shape[0]
    reach = size_gy // stages

    def along_z(step):
        place = lax.rem(own * size_gy + gy + step + 2 * size_gy, 2 * size_gy)
        return ((place // size_gy) * half + x, lax.rem(place, size_gy), gz)

    x_right = (own * half + lax.rem(x + 1, half), gy, gz)
    x_left = (own * half + lax.rem(x + half - 1, half), gy, gz)
    y_up, y_down = (gx, gy + 1, gz), (gx, gy - 1, gz)
    z_up, z_down = (gx, gy, gz + 1), (gx, gy, gz - 1)
    has_y_up, has_y_down = gy < size_gy - 1, gy > 0
    has_z_up, has_z_down = gz < size_gz - 1, gz > 0
    optional = ((has_y_up, y_up), (has_y_down, y_down), (has_z_up, z_up), (has_z_down, z_down))

    def zero(ref):
        ref[...] = jnp.zeros_like(ref)

    for ref in (*xs, hy, sy, hz, sz):
        zero(ref)

    barrier = pltpu.get_barrier_semaphore()
    for device in (x_right, x_left, along_z(reach), along_z(-reach)):
        pl.semaphore_signal(barrier, inc=1, device_id=device, device_id_type=MESH)
    for there, device in optional:
        @pl.when(there)
        def _():
            pl.semaphore_signal(barrier, inc=1, device_id=device, device_id_type=MESH)
    count = 4
    for there, _ in optional:
        count = count + there.astype(jnp.int32)
    pl.semaphore_wait(barrier, count)

    part = 8 // CHUNKS

    def relay(stage, way, chunk):
        first, slots = ((right_ref, relay_b), (coef_ref, relay_k))[way]
        rows = pl.ds(chunk * part, part)
        source = first.at[rows] if stage == 0 else slots.at[stage - 1, rows]
        return pltpu.make_async_remote_copy(
            src_ref=source, dst_ref=slots.at[stage, rows],
            send_sem=relay_send.at[stage, way, chunk], recv_sem=relay_recv.at[stage, way, chunk],
            device_id=along_z(reach if way == 0 else -reach), device_id_type=MESH)

    for stage in range(stages):
        for chunk in range(CHUNKS):
            for way in range(2):
                if stage:
                    relay(stage - 1, way, chunk).wait_recv()
                relay(stage, way, chunk).start()
    for chunk in range(CHUNKS):
        for way in range(2):
            relay(stages - 1, way, chunk).wait_recv()
    for stage in range(stages):
        for chunk in range(CHUNKS):
            for way in range(2):
                relay(stage, way, chunk).wait_send()

    row = lax.broadcasted_iota(jnp.int32, (16, 128), 0)
    lane = lax.broadcasted_iota(jnp.int32, (16, 128), 1)

    def remote(level, par, index, source, target, device):
        return pltpu.make_async_remote_copy(
            src_ref=source, dst_ref=target, send_sem=send_sem.at[level, par, index[0]],
            recv_sem=recv_sem.at[level, par, index[1]], device_id=device, device_id_type=MESH)

    def planes(level):
        return xs[level].shape[2] - 2

    def copies(level, par):
        n = planes(level)
        buf = xs[level]
        over = (x == half - 1).astype(jnp.int32)
        under = (x > 0).astype(jnp.int32)
        used = max(8, 2 * n)
        rows = pl.ds(0, used)
        right = (
            (None, remote(level, par, (0, over), buf.at[par, 0, n], buf.at[par, over, 0], x_right)),
            (x < half - 1, remote(level, par, (1, 1), buf.at[par, 1, n], buf.at[par, 1, 0], x_right)),
            (None, remote(level, par, (2, 2 + under), buf.at[par, 1, 1], buf.at[par, under, n + 1], x_left)),
            (x > 0, remote(level, par, (3, 2), buf.at[par, 0, 1], buf.at[par, 0, n + 1], x_left)),
            (has_y_up, remote(level, par, (4, 4), sy.at[level, par, 0, rows], hy.at[level, par, 0, rows], y_up)),
            (has_y_down, remote(level, par, (5, 5), sy.at[level, par, 1, rows], hy.at[level, par, 1, rows], y_down)),
            (has_z_up, remote(level, par, (6, 6), sz.at[level, par, 0], hz.at[level, par, 0], z_up)),
            (has_z_down, remote(level, par, (7, 7), sz.at[level, par, 1], hz.at[level, par, 1], z_down)),
        )
        arrive = (
            (x > 0, remote(level, par, (0, 0), buf.at[par, 0, n], buf.at[par, 0, 0], x_right)),
            (None, remote(level, par, (1, 1), buf.at[par, 1, n], buf.at[par, 1, 0], x_right)),
            (None, remote(level, par, (3, 2), buf.at[par, 0, 1], buf.at[par, 0, n + 1], x_left)),
            (x < half - 1, remote(level, par, (2, 3), buf.at[par, 1, 1], buf.at[par, 1, n + 1], x_left)),
            (has_y_down, right[4][1]),
            (has_y_up, right[5][1]),
            (has_z_down, right[6][1]),
            (has_z_up, right[7][1]),
        )
        return right, arrive

    def each(listed, act):
        for there, copy in listed:
            if there is None:
                act(copy)
            else:
                @pl.when(there)
                def _():
                    act(copy)

    def start(level, par):
        n, w = planes(level), 2**level
        buf = xs[level]
        to_up, to_down = jnp.zeros((16, 128), jnp.float32), jnp.zeros((16, 128), jnp.float32)
        for s in range(2):
            sy[level, par, 0, s * n : (s + 1) * n, :] = buf[par, s, 1 : n + 1, 15, :]
            sy[level, par, 1, s * n : (s + 1) * n, :] = buf[par, s, 1 : n + 1, 0, :]
            for p in range(n):
                at = (s * n + p) * w
                here = (lane >= at) & (lane < at + w)
                value = buf[par, s, 1 + p]
                to_up = jnp.where(here, pltpu.roll(value, (at + w) % 128, 1), to_up)
                to_down = jnp.where(here, pltpu.roll(value, at, 1), to_down)
        sz[level, par, 0] = to_up
        sz[level, par, 1] = to_down
        each(copies(level, par)[0], lambda copy: copy.start())

    def finish(level, par):
        sent, arrive = copies(level, par)
        each(arrive, lambda copy: copy.wait_recv())
        each(sent, lambda copy: copy.wait_send())

    def neighbours(level, par, s):
        n, w = planes(level), 2**level
        buf = xs[level]
        value = buf[par, s, 1 : n + 1]
        low, high = hz[level, par, 0], hz[level, par, 1]
        shape = (n, 16, 128)
        lows = jnp.stack([pltpu.roll(low, (128 - (s * n + p) * w) % 128, 1) for p in range(n)])
        highs = jnp.stack([pltpu.roll(high, (128 - w - (s * n + p) * w) % 128, 1) for p in range(n)])
        under = jnp.broadcast_to(hy[level, par, 0, s * n : (s + 1) * n, :][:, None, :], shape)
        over = jnp.broadcast_to(hy[level, par, 1, s * n : (s + 1) * n, :][:, None, :], shape)
        return value, (
            buf[par, s, 0:n],
            buf[par, s, 2 : n + 2],
            jnp.where(row < w, under, pltpu.roll(value, w, 1)),
            jnp.where(row >= 16 - w, over, pltpu.roll(value, 16 - w, 1)),
            jnp.where(lane < w, lows, pltpu.roll(value, w, 2)),
            jnp.where(lane >= 128 - w, highs, pltpu.roll(value, 128 - w, 2)),
        )

    def scaled_residual(level, par, s):
        value, around = neighbours(level, par, s)
        total = bs[level][s] - value
        for i in range(6):
            total = total + gs[level][i, s] * around[i]
        return value, total

    def inside(level):
        return slice(1, planes(level) + 1)

    state = {"par": 0}

    def smooth(level, fresh):
        keep = inside(level)
        rho = 1.0 / SIGMA
        par = state["par"]
        if fresh:
            for s in range(2):
                u = bs[level][s] * (1.0 / CENTRE)
                us[level][s] = u
                xs[level][par, s, keep] = u
            sweeps = [None]
        else:
            sweeps = [(None, 1.0 / CENTRE)]
        sweeps = [] if fresh else [(0.0, 1.0 / CENTRE)]
        for _ in range(DEGREE - 1):
            rho_next = 1.0 / (2.0 * SIGMA - rho)
            sweeps.append((rho_next * rho, 2.0 * rho_next / HALF))
            rho = rho_next
        for old, new in sweeps:
            start(level, par)
            finish(level, par)
            for s in range(2):
                value, total = scaled_residual(level, par, s)
                u = new * total
                if old:
                    u = old * us[level][s] + u
                us[level][s] = u
                xs[level][1 - par, s, keep] = value + u
            par = 1 - par
        state["par"] = par

    def pair_sum(value, w):
        even_row = lax.rem(row, 2 * w) < w
        value = value + jnp.where(even_row, pltpu.roll(value, 16 - w, 1), pltpu.roll(value, w, 1))
        even_lane = lax.rem(lane, 2 * w) < w
        return value + jnp.where(even_lane, pltpu.roll(value, 128 - w, 2), pltpu.roll(value, w, 2))

    def restrict(value, w):
        total = pair_sum(value, w)
        return jnp.stack([total[2 * p] + total[2 * p + 1] for p in range(value.shape[0] // 2)]) * 0.125

    for level in range(3):
        n = planes(level)
        if level == 0:
            xs[0][0, own, 1 : n + 1] = coef_ref[...]
            xs[0][0, 1 - own, 1 : n + 1] = relay_k[stages - 1]
            bs[0][own] = right_ref[...]
            bs[0][1 - own] = relay_b[stages - 1]
        else:
            for s in range(2):
                xs[level][0, s, 1 : n + 1] = restrict(xs[level - 1][0, s, 1 : 2 * n + 1], 2 ** (level - 1))
        start(level, 0)
    for level in range(3):
        finish(level, 0)
        for s in range(2):
            value, around = neighbours(level, 0, s)
            faces = [0.5 * (value + other) for other in around]
            diagonal = faces[0]
            for face in faces[1:]:
                diagonal = diagonal + face
            inverse = 1.0 / diagonal
            for i in range(6):
                gs[level][i, s] = faces[i] * inverse
            ds[level][0, s] = diagonal * 0.25**level
            ds[level][1, s] = inverse * 4.0**level
    state["par"] = 1
    for s in range(2):
        bs[0][s] = bs[0][s] * ds[0][1, s]

    def down(level):
        par = state["par"]
        start(level, par)
        finish(level, par)
        for s in range(2):
            _, total = scaled_residual(level, par, s)
            coarse = restrict(total * ds[level][0, s], 2**level)
            bs[level + 1][s] = coarse * ds[level + 1][1, s]
        held = par
        state["par"] = 1 - par
        return held

    def correct(level, held):
        keep, coarse = inside(level), xs[level + 1]
        par = state["par"]
        for s in range(2):
            fine = xs[level][held, s, keep]
            add = coarse[par, s, inside(level + 1)]
            n = fine.shape[0] // 2
            wide = jnp.stack([add[p // 2] for p in range(2 * n)])
            xs[level][par, s, keep] = fine + wide

    smooth(0, True)
    held0 = down(0)
    smooth(1, True)
    held1 = down(1)
    smooth(2, True)
    correct(1, held1)
    smooth(1, False)
    correct(0, held0)
    smooth(0, False)
    par = state["par"]
    start(0, par)
    finish(0, par)
    for s in range(2):
        @pl.when(own == s)
        def _():
            value, total = scaled_residual(0, par, s)
            sol_ref[...] = value
            res_ref[...] = total * ds[0][0, s]


def solution(mesh):
    sizes = tuple(mesh.shape[a] for a in ("gx", "gy", "gz"))
    stages = 4 if sizes[1] % 4 == 0 else sizes[1]
    vmem = pltpu.VMEM
    f32 = jnp.float32
    levels = (8, 4, 2)
    scratch = (
        [vmem((2, 2, n + 2, 16, 128), f32) for n in levels]
        + [vmem((6, 2, n, 16, 128), f32) for n in levels]
        + [vmem((2, n, 16, 128), f32) for n in levels]
        + [vmem((2, n, 16, 128), f32) for n in levels]
        + [vmem((2, 2, n, 16, 128), f32) for n in levels]
        + [vmem((3, 2, 2, 16, 128), f32)] * 4
        + [vmem((stages, 8, 16, 128), f32)] * 2
        + [pltpu.SemaphoreType.DMA((3, 2, 8))] * 2
        + [pltpu.SemaphoreType.DMA((stages, 2, CHUNKS))] * 2
    )

    def per_device(right_side, coefficient):
        return pl.pallas_call(
            functools.partial(kernel, sizes),
            out_shape=(jax.ShapeDtypeStruct((8, 16, 128), f32),) * 2,
            in_specs=[pl.BlockSpec(memory_space=vmem)] * 2,
            out_specs=(pl.BlockSpec(memory_space=vmem),) * 2,
            scratch_shapes=scratch,
            compiler_params=pltpu.CompilerParams(collective_id=0, has_side_effects=True),
            name="vcycle",
        )(right_side, coefficient)

    specs = (P("gx", "gy", "gz"), P("gx", "gy", "gz"))
    return jax.shard_map(per_device, mesh=mesh, in_specs=specs, out_specs=specs, check_vma=False)
```

time: 1050 us -> 132 us (0.13)
  the two profiles are of different devices: /device:TPU:14 before, /device:TPU:1 now
where the time goes in v1:
time: 132 us
  Pallas kernels  129 us (98%)
  local copies, waits for them, and re-layouts  2.14 us (2%)
    pallas_call x1, Pallas kernels, per_device(): pl.pallas_call(functools.partial(kernel, sizes), out_shape=(jax.ShapeDtyp...  129 us

profile of v1, /device:TPU:1, one launch (start us, length us, event | category | flops | bytes accessed | tf_op | source)
XLA Modules:
  0.0 131.7 jit_solution(9950502141923887445)
XLA Ops:
  0.6 128.9 %vcycle.1 = (f32[8,16,128]{2,1,0:T(8,128)}, f32[8,16,128]{2,1,0:T(8,128)}) custom-call(f32[8,16,128]{2,1,0:T(8,128)} %right_ref.1, f32[8,16,128]{2,1,0:T(8,128)} %coef_ref.1), custom_call_target="tpu_custom_call" | custom-call | tf_op jit(solution)/shard_map/vcycle/pallas_call | solution.py:318
  129.5 0.0 copy-start
  129.6 1.5 %copy.6 = f32[8,16,128]{2,1,0:T(8,128)} copy(f32[8,16,128]{2,1,0:T(8,128)} %get-tuple-element.4) | data formatting | bytes 131072
  131.1 0.0 copy-done
  131.1 0.6 copy.7
Async XLA Ops:
  129.5 1.5 %copy-start = (f32[8,16,128]{2,1,0:T(8,128)S(1)}, f32[8,16,128]{2,1,0:T(8,128)}, u32[]{:S(2)}) copy-start(f32[8,16,128]{2,1,0:T(8,128)} %get-tuple-element.5) | copy-start | bytes 196612

commit v2 on v1

--- a/solution.py
+++ b/solution.py
@@ -18,9 +18,10 @@
 
 
 def kernel(sizes, right_ref, coef_ref, sol_ref, res_ref, *scratch):
-    (x0, x1, x2, g0, g1, g2, u0, u1, u2, b0, b1, b2, d0, d1, d2, hy, sy, hz, sz,
-     relay_b, relay_k, send_sem, recv_sem, relay_send, relay_recv) = scratch
-    xs, gs, us, bs, ds = (x0, x1, x2), (g0, g1, g2), (u0, u1, u2), (b0, b1, b2), (d0, d1, d2)
+    (x0, g0, u0, b0, d0, hy, sy, hz, sz, relay_b, relay_k, send_sem, recv_sem, relay_send, relay_recv,
+     k1, r1, x1a, x1b, x1s, g1, u1, d1, k2, r2, x2a, x2b, g2, u2, d2, wide, zs, zr,
+     gather_send, gather_recv, cross_send, cross_recv) = scratch
+    xs, gs, us, bs, ds = (x0,), (g0,), (u0,), (b0,), (d0,)
     size_gx, size_gy, size_gz = sizes
     half = size_gx // 2
     gx, gy, gz = lax.axis_index("gx"), lax.axis_index("gy"), lax.axis_index("gz")
@@ -44,18 +45,27 @@
     def zero(ref):
         ref[...] = jnp.zeros_like(ref)
 
-    for ref in (*xs, hy, sy, hz, sz):
+    for ref in (*xs, hy, sy, hz, sz, k1, r1, x1s, r2, zs, zr):
         zero(ref)
 
     barrier = pltpu.get_barrier_semaphore()
     for device in (x_right, x_left, along_z(reach), along_z(-reach)):
         pl.semaphore_signal(barrier, inc=1, device_id=device, device_id_type=MESH)
-    for there, device in optional:
+    corners = (
+        (has_y_up & has_z_up, (gx, gy + 1, gz + 1)),
+        (has_y_up & has_z_down, (gx, gy + 1, gz - 1)),
+        (has_y_down & has_z_up, (gx, gy - 1, gz + 1)),
+        (has_y_down & has_z_down, (gx, gy - 1, gz - 1)),
+    )
+    for there, device in (*optional, *corners):
         @pl.when(there)
         def _():
             pl.semaphore_signal(barrier, inc=1, device_id=device, device_id_type=MESH)
-    count = 4
-    for there, _ in optional:
+    count = 2 + max(half - 1, 2)
+    for step in range(2, half - 1):
+        device = (own * half + lax.rem(x + step, half), gy, gz)
+        pl.semaphore_signal(barrier, inc=1, device_id=device, device_id_type=MESH)
+    for there, _ in (*optional, *corners):
         count = count + there.astype(jnp.int32)
     pl.semaphore_wait(barrier, count)
 
@@ -186,7 +196,7 @@
 
     state = {"par": 0}
 
-    def smooth(level, fresh):
+    def smooth(level, fresh, between=None):
         keep = inside(level)
         rho = 1.0 / SIGMA
         par = state["par"]
@@ -195,16 +205,15 @@
                 u = bs[level][s] * (1.0 / CENTRE)
                 us[level][s] = u
                 xs[level][par, s, keep] = u
-            sweeps = [None]
-        else:
-            sweeps = [(None, 1.0 / CENTRE)]
         sweeps = [] if fresh else [(0.0, 1.0 / CENTRE)]
         for _ in range(DEGREE - 1):
             rho_next = 1.0 / (2.0 * SIGMA - rho)
             sweeps.append((rho_next * rho, 2.0 * rho_next / HALF))
             rho = rho_next
-        for old, new in sweeps:
+        for number, (old, new) in enumerate(sweeps):
             start(level, par)
+            if between:
+                between(number)
             finish(level, par)
             for s in range(2):
                 value, total = scaled_residual(level, par, s)
@@ -226,64 +235,239 @@
         total = pair_sum(value, w)
         return jnp.stack([total[2 * p] + total[2 * p + 1] for p in range(value.shape[0] // 2)]) * 0.125
 
-    for level in range(3):
-        n = planes(level)
-        if level == 0:
-            xs[0][0, own, 1 : n + 1] = coef_ref[...]
-            xs[0][0, 1 - own, 1 : n + 1] = relay_k[stages - 1]
-            bs[0][own] = right_ref[...]
-            bs[0][1 - own] = relay_b[stages - 1]
-        else:
-            for s in range(2):
-                xs[level][0, s, 1 : n + 1] = restrict(xs[level - 1][0, s, 1 : 2 * n + 1], 2 ** (level - 1))
-        start(level, 0)
-    for level in range(3):
-        finish(level, 0)
+    count1, count2 = 4 * half, 2 * half
+    wide_row = lax.broadcasted_iota(jnp.int32, (24, 256), 0)
+    wide_lane = lax.broadcasted_iota(jnp.int32, (24, 256), 1)
+    odd = lax.rem(wide_lane, 2) == 1
+    lane8 = lax.broadcasted_iota(jnp.int32, (8, 128), 1)
+    odd8 = lax.rem(lane8, 2) == 1
+    mine, owned = slice(0, 8), slice(0, 128)
+
+    def gather_copy(which, ref, base, step):
+        part_of = pl.ds(base + 4 * x, 4)
+        return pltpu.make_async_remote_copy(
+            src_ref=ref.at[part_of, mine, owned], dst_ref=ref.at[part_of, mine, owned],
+            send_sem=gather_send.at[which, step], recv_sem=gather_recv.at[which, step],
+            device_id=(own * half + lax.rem(x + step, half), gy, gz), device_id_type=MESH)
+
+    def gather_start(which, ref, base, values):
         for s in range(2):
-            value, around = neighbours(level, 0, s)
+            wide[s] = values[s]
+        for p in range(4):
+            low, high = wide[0, p, pl.ds(0, 8, stride=2), :], wide[1, p, pl.ds(0, 8, stride=2), :]
+            ref[base + 4 * x + p, mine, owned] = jnp.where(odd8, high, low)
+        for step in range(1, half):
+            gather_copy(which, ref, base, step).start()
+
+    def gather_finish(which, ref, base):
+        for step in range(1, half):
+            source = lax.rem(x + half - step, half)
+            part_of = pl.ds(base + 4 * source, 4)
+            pltpu.make_async_remote_copy(
+                src_ref=ref.at[part_of, mine, owned], dst_ref=ref.at[part_of, mine, owned],
+                send_sem=gather_send.at[which, step], recv_sem=gather_recv.at[which, step],
+                device_id=(own * half + lax.rem(x + step, half), gy, gz), device_id_type=MESH).wait_recv()
+        for step in range(1, half):
+            gather_copy(which, ref, base, step).wait_send()
+
+    def cross_copies(stage, ref, base, number):
+        tiles = pl.ds(0, max(1, number // 8))
+        body = slice(base, base + number)
+
+        def to(index, source, target, device):
+            return pltpu.make_async_remote_copy(
+                src_ref=source, dst_ref=target, send_sem=cross_send.at[stage, index],
+                recv_sem=cross_recv.at[stage, index], device_id=device, device_id_type=MESH)
+
+        def pack(index, side, block, device):
+            return to(index, zs.at[stage, side, tiles], zr.at[stage, side, block, tiles], device)
+
+        block = ref.at[body, mine, owned]
+        sent = (
+            (has_y_up, to(0, block, ref.at[body, 16:24, owned], y_up)),
+            (has_y_down, to(1, block, ref.at[body, 8:16, owned], y_down)),
+            (has_z_up, pack(2, 0, 0, z_up)),
+            (has_z_down, pack(3, 1, 0, z_down)),
+            (corners[0][0], pack(4, 0, 2, corners[0][1])),
+            (corners[1][0], pack(5, 1, 2, corners[1][1])),
+            (corners[2][0], pack(6, 0, 1, corners[2][1])),
+            (corners[3][0], pack(7, 1, 1, corners[3][1])),
+        )
+        opposite = (has_y_down, has_y_up, has_z_down, has_z_up,
+                    corners[3][0], corners[2][0], corners[1][0], corners[0][0])
+        arrive = tuple((there, sent[i][1]) for i, there in enumerate(opposite))
+        return sent, arrive
+
+    def cross_start(stage, ref, base, number):
+        for t in range(max(1, number // 8)):
+            high, low = jnp.zeros((8, 128), jnp.float32), jnp.zeros((8, 128), jnp.float32)
+            for i in range(min(8, number)):
+                value = ref[base + 8 * t + i, mine, owned]
+                here = (lane8 >= 16 * i) & (lane8 < 16 * i + 16)
+                high = jnp.where(here, pltpu.roll(value, (16 * i + 16) % 128, 1), high)
+                low = jnp.where(here, pltpu.roll(value, 16 * i, 1), low)
+            zs[stage, 0, t] = high
+            zs[stage, 1, t] = low
+        each(cross_copies(stage, ref, base, number)[0], lambda copy: copy.start())
+
+    def cross_finish(stage, ref, base, number):
+        sent, arrive = cross_copies(stage, ref, base, number)
+        each(arrive, lambda copy: copy.wait_recv())
+        each(sent, lambda copy: copy.wait_send())
+        for t in range(max(1, number // 8)):
+            for block in range(3):
+                below, above = zr[stage, 0, block, t], zr[stage, 1, block, t]
+                for i in range(min(8, number)):
+                    ref[base + 8 * t + i, 8 * block : 8 * block + 8, 128:256] = jnp.where(
+                        lane8 < 16, pltpu.roll(above, (128 - 16 * i) % 128, 1),
+                        jnp.where(lane8 >= 112, pltpu.roll(below, (112 - 16 * i) % 128, 1), 0.0))
+
+    def edges(ref, number):
+        ref[0] = jnp.where(odd, pltpu.roll(ref[number], 1, 1), 0.0)
+        ref[number + 1] = jnp.where(odd, 0.0, pltpu.roll(ref[1], 255, 1))
+
+    GROUP = 2
+
+    def groups(number):
+        return [(a, a + GROUP) for a in range(0, number, GROUP)]
+
+    def spread(ref, a, b, level):
+        w = level
+        value = ref[1 + a : 1 + b]
+        return value, (
+            ref[a:b], ref[a + 2 : b + 2],
+            pltpu.roll(value, w, 1), pltpu.roll(value, 24 - w, 1),
+            pltpu.roll(value, 2 * w, 2), pltpu.roll(value, 256 - 2 * w, 2),
+        )
+
+    def coarse_faces(level, ref, number, gref, dref):
+        edges(ref, number)
+        for a, b in groups(number):
+            value, around = spread(ref, a, b, level)
             faces = [0.5 * (value + other) for other in around]
             diagonal = faces[0]
             for face in faces[1:]:
                 diagonal = diagonal + face
-            inverse = 1.0 / diagonal
+            inverse = jnp.where(value > 0.0, 1.0 / diagonal, 0.0)
             for i in range(6):
-                gs[level][i, s] = faces[i] * inverse
-            ds[level][0, s] = diagonal * 0.25**level
-            ds[level][1, s] = inverse * 4.0**level
+                gref[i, a:b] = faces[i] * inverse
+            dref[0, a:b] = diagonal * 0.25**level
+            dref[1, a:b] = inverse * 4.0**level
+
+    def coarse_total(level, ref, a, b, right, gref):
+        value, around = spread(ref, a, b, level)
+        total = right[a:b] - value
+        for i in range(6):
+            total = total + gref[i, a:b] * around[i]
+        return value, total
+
+    def coarse_smooth(level, begin, buffers, number, right, gref, uref):
+        rho = 1.0 / SIGMA
+        now, sweeps = begin, []
+        if begin is None:
+            now, buffers = buffers[0], buffers[1:] + buffers[:1]
+            for a, b in groups(number):
+                u = right[a:b] * (1.0 / CENTRE)
+                uref[a:b] = u
+                now[1 + a : 1 + b] = u
+        else:
+            sweeps = [(0.0, 1.0 / CENTRE)]
+        for _ in range(DEGREE - 1):
+            rho_next = 1.0 / (2.0 * SIGMA - rho)
+            sweeps.append((rho_next * rho, 2.0 * rho_next / HALF))
+            rho = rho_next
+        for old, new in sweeps:
+            then, buffers = buffers[0], buffers[1:] + buffers[:1]
+            edges(now, number)
+            for a, b in groups(number):
+                value, total = coarse_total(level, now, a, b, right, gref)
+                u = new * total
+                if old:
+                    u = old * uref[a:b] + u
+                uref[a:b] = u
+                then[1 + a : 1 + b] = value + u
+            now = then
+        return now
+
+    def coarse_restrict(pairs):
+        value = pairs[0] + pairs[1]
+        value = value + jnp.where(lax.rem(wide_row, 2) == 0, pltpu.roll(value, 23, 0), pltpu.roll(value, 1, 0))
+        value = value + jnp.where(lax.rem(wide_lane, 4) < 2, pltpu.roll(value, 254, 1), pltpu.roll(value, 2, 1))
+        return value * 0.125
+
+    xs[0][0, own, 1:9] = coef_ref[...]
+    xs[0][0, 1 - own, 1:9] = relay_k[stages - 1]
+    bs[0][own] = right_ref[...]
+    bs[0][1 - own] = relay_b[stages - 1]
+    start(0, 0)
+    gather_start(0, k1, 1, [restrict(xs[0][0, s, 1:9], 1) for s in range(2)])
+    finish(0, 0)
+    for s in range(2):
+        value, around = neighbours(0, 0, s)
+        faces = [0.5 * (value + other) for other in around]
+        diagonal = faces[0]
+        for face in faces[1:]:
+            diagonal = diagonal + face
+        inverse = 1.0 / diagonal
+        for i in range(6):
+            gs[0][i, s] = faces[i] * inverse
+        ds[0][0, s] = diagonal
+        ds[0][1, s] = inverse
+        bs[0][s] = bs[0][s] * inverse
     state["par"] = 1
+
+    def between(sweep):
+        if sweep == 0:
+            gather_finish(0, k1, 1)
+            cross_start(0, k1, 1, count1)
+        if sweep == 1:
+            cross_finish(0, k1, 1, count1)
+            coarse_faces(1, k1, count1, g1, d1)
+        if sweep == 2:
+            for m in range(count2):
+                k2[1 + m] = coarse_restrict(k1[1 + 2 * m : 3 + 2 * m])
+            coarse_faces(2, k2, count2, g2, d2)
+
+    smooth(0, True, between)
+    held = state["par"]
+    start(0, held)
+    finish(0, held)
+    fine = []
     for s in range(2):
-        bs[0][s] = bs[0][s] * ds[0][1, s]
-
-    def down(level):
-        par = state["par"]
-        start(level, par)
-        finish(level, par)
+        _, total = scaled_residual(0, held, s)
+        fine.append(restrict(total * ds[0][0, s], 1))
+    gather_start(1, r1, 0, fine)
+    gather_finish(1, r1, 0)
+    cross_start(1, r1, 0, count1)
+    cross_finish(1, r1, 0, count1)
+    for a, b in groups(count1):
+        r1[a:b] = r1[a:b] * d1[1, a:b]
+    now = coarse_smooth(1, None, [x1a, x1b], count1, r1, g1, u1)
+    edges(now, count1)
+    for m in range(count2):
+        _, total = coarse_total(1, now, 2 * m, 2 * m + 2, r1, g1)
+        r2[m, mine, owned] = coarse_restrict(total * d1[0, 2 * m : 2 * m + 2])[mine, owned]
+    cross_start(2, r2, 0, count2)
+    cross_finish(2, r2, 0, count2)
+    for a, b in groups(count2):
+        r2[a:b] = r2[a:b] * d2[1, a:b]
+    deep = coarse_smooth(2, None, [x2a, x2b], count2, r2, g2, u2)
+    for q in range(count1):
+        x1s[1 + q, mine, owned] = now[1 + q, mine, owned] + deep[1 + q // 2, mine, owned]
+    cross_start(3, x1s, 1, count1)
+    cross_finish(3, x1s, 1, count1)
+    now = coarse_smooth(1, x1s, [x1a, x1b], count1, r1, g1, u1)
+    par = 1 - held
+    for p in range(4):
+        value = now[1 + 4 * x + p, mine, owned]
         for s in range(2):
-            _, total = scaled_residual(level, par, s)
-            coarse = restrict(total * ds[level][0, s], 2**level)
-            bs[level + 1][s] = coarse * ds[level + 1][1, s]
-        held = par
-        state["par"] = 1 - par
-        return held
-
-    def correct(level, held):
-        keep, coarse = inside(level), xs[level + 1]
-        par = state["par"]
-        for s in range(2):
-            fine = xs[level][held, s, keep]
-            add = coarse[par, s, inside(level + 1)]
-            n = fine.shape[0] // 2
-            wide = jnp.stack([add[p // 2] for p in range(2 * n)])
-            xs[level][par, s, keep] = fine + wide
-
-    smooth(0, True)
-    held0 = down(0)
-    smooth(1, True)
-    held1 = down(1)
-    smooth(2, True)
-    correct(1, held1)
-    smooth(1, False)
-    correct(0, held0)
+            half_of = jnp.where(odd8, value, pltpu.roll(value, 127, 1)) if s else jnp.where(odd8, pltpu.roll(value, 1, 1), value)
+            wide[s, p, pl.ds(0, 8, stride=2), :] = half_of
+            wide[s, p, pl.ds(1, 8, stride=2), :] = half_of
+    for s in range(2):
+        for p in range(8):
+            xs[0][par, s, 1 + p] = xs[0][held, s, 1 + p] + wide[s, p // 2]
+    state["par"] = par
     smooth(0, False)
     par = state["par"]
     start(0, par)
@@ -301,18 +485,24 @@
     stages = 4 if sizes[1] % 4 == 0 else sizes[1]
     vmem = pltpu.VMEM
     f32 = jnp.float32
-    levels = (8, 4, 2)
-    scratch = (
-        [vmem((2, 2, n + 2, 16, 128), f32) for n in levels]
-        + [vmem((6, 2, n, 16, 128), f32) for n in levels]
-        + [vmem((2, n, 16, 128), f32) for n in levels]
-        + [vmem((2, n, 16, 128), f32) for n in levels]
-        + [vmem((2, 2, n, 16, 128), f32) for n in levels]
-        + [vmem((3, 2, 2, 16, 128), f32)] * 4
-        + [vmem((stages, 8, 16, 128), f32)] * 2
-        + [pltpu.SemaphoreType.DMA((3, 2, 8))] * 2
-        + [pltpu.SemaphoreType.DMA((stages, 2, CHUNKS))] * 2
-    )
+    half = sizes[0] // 2
+    n1, n2 = 4 * half, 2 * half
+    dma = pltpu.SemaphoreType.DMA
+
+    def big(*lead):
+        return vmem((*lead, 24, 256), f32)
+
+    scratch = [
+        vmem((2, 2, 10, 16, 128), f32), vmem((6, 2, 8, 16, 128), f32), vmem((2, 8, 16, 128), f32),
+        vmem((2, 8, 16, 128), f32), vmem((2, 2, 8, 16, 128), f32),
+        *[vmem((1, 2, 2, 16, 128), f32)] * 4,
+        *[vmem((stages, 8, 16, 128), f32)] * 2,
+        *[dma((1, 2, 8))] * 2, *[dma((stages, 2, CHUNKS))] * 2,
+        big(n1 + 2), big(n1), big(n1 + 2), big(n1 + 2), big(n1 + 2), big(6, n1), big(n1), big(2, n1),
+        big(n2 + 2), big(n2), big(n2 + 2), big(n2 + 2), big(6, n2), big(n2), big(2, n2),
+        vmem((2, 4, 16, 128), f32), vmem((4, 2, 2, 8, 128), f32), vmem((4, 2, 3, 2, 8, 128), f32),
+        *[dma((2, half))] * 2, *[dma((4, 8))] * 2,
+    ]
 
     def per_device(right_side, coefficient):
         return pl.pallas_call(

time: 132 us -> 115 us (0.87)
  Pallas kernels: 129 us -> 112 us
    pallas_call x1, Pallas kernels: 129 us -> 112 us  [per_device(): pl.pallas_call(functools.partial(kernel, sizes), out_shape=(jax.ShapeDtyp...]
where the time goes in v2:
time: 115 us
  Pallas kernels  112 us (97%)
  local copies, waits for them, and re-layouts  2.14 us (2%)
    pallas_call x1, Pallas kernels, per_device(): pl.pallas_call(functools.partial(kernel, sizes), out_shape=(jax.ShapeDtyp...  112 us

profile of v2, /device:TPU:1, one launch (start us, length us, event | category | flops | bytes accessed | tf_op | source)
XLA Modules:
  0.0 115.2 jit_solution(10160481805875114546)
XLA Ops:
  0.6 112.4 %vcycle.1 = (f32[8,16,128]{2,1,0:T(8,128)}, f32[8,16,128]{2,1,0:T(8,128)}) custom-call(f32[8,16,128]{2,1,0:T(8,128)} %right_ref.1, f32[8,16,128]{2,1,0:T(8,128)} %coef_ref.1), custom_call_target="tpu_custom_call" | custom-call | tf_op jit(solution)/shard_map/vcycle/pallas_call | solution.py:508
  113.0 0.0 copy-start
  113.0 1.5 %copy.6 = f32[8,16,128]{2,1,0:T(8,128)} copy(f32[8,16,128]{2,1,0:T(8,128)} %get-tuple-element.4) | data formatting | bytes 131072
  114.5 0.0 copy-done
  114.6 0.6 copy.7
Async XLA Ops:
  113.0 1.5 %copy-start = (f32[8,16,128]{2,1,0:T(8,128)S(1)}, f32[8,16,128]{2,1,0:T(8,128)}, u32[]{:S(2)}) copy-start(f32[8,16,128]{2,1,0:T(8,128)} %get-tuple-element.5) | copy-start | bytes 196612

commit v3 on v2

--- a/solution.py
+++ b/solution.py
@@ -14,25 +14,21 @@
 HALF = 0.5 * (cheb_high - cheb_low)
 SIGMA = CENTRE / HALF
 MESH = pl.DeviceIdType.MESH
-CHUNKS = 2
 
 
 def kernel(sizes, right_ref, coef_ref, sol_ref, res_ref, *scratch):
     (x0, g0, u0, b0, d0, hy, sy, hz, sz, relay_b, relay_k, send_sem, recv_sem, relay_send, relay_recv,
      k1, r1, x1a, x1b, x1s, g1, u1, d1, k2, r2, x2a, x2b, g2, u2, d2, wide, zs, zr,
-     gather_send, gather_recv, cross_send, cross_recv) = scratch
+     gather_send, gather_recv, cross_send, cross_recv,
+     ek, eb, exa, exb, eg, eu, ez, er, side_send, side_recv, deep_send, deep_recv, spill) = scratch
     xs, gs, us, bs, ds = (x0,), (g0,), (u0,), (b0,), (d0,)
     size_gx, size_gy, size_gz = sizes
     half = size_gx // 2
     gx, gy, gz = lax.axis_index("gx"), lax.axis_index("gy"), lax.axis_index("gz")
     own = gx // half
     x = gx % half
-    stages = relay_b.shape[0]
-    reach = size_gy // stages
-
-    def along_z(step):
-        place = lax.rem(own * size_gy + gy + step + 2 * size_gy, 2 * size_gy)
-        return ((place // size_gy) * half + x, lax.rem(place, size_gy), gz)
+
+    across = ((1 - own) * half + x, gy, gz)
 
     x_right = (own * half + lax.rem(x + 1, half), gy, gz)
     x_left = (own * half + lax.rem(x + half - 1, half), gy, gz)
@@ -45,11 +41,11 @@
     def zero(ref):
         ref[...] = jnp.zeros_like(ref)
 
-    for ref in (*xs, hy, sy, hz, sz, k1, r1, x1s, r2, zs, zr):
+    for ref in (*xs, hy, sy, hz, sz, k1, r1, x1s, r2, zs, zr, ek, eb, exa, er):
         zero(ref)
 
     barrier = pltpu.get_barrier_semaphore()
-    for device in (x_right, x_left, along_z(reach), along_z(-reach)):
+    for device in (x_right, x_left, across):
         pl.semaphore_signal(barrier, inc=1, device_id=device, device_id_type=MESH)
     corners = (
         (has_y_up & has_z_up, (gx, gy + 1, gz + 1)),
@@ -61,7 +57,7 @@
         @pl.when(there)
         def _():
             pl.semaphore_signal(barrier, inc=1, device_id=device, device_id_type=MESH)
-    count = 2 + max(half - 1, 2)
+    count = 1 + max(half - 1, 2)
     for step in range(2, half - 1):
         device = (own * half + lax.rem(x + step, half), gy, gz)
         pl.semaphore_signal(barrier, inc=1, device_id=device, device_id_type=MESH)
@@ -69,30 +65,15 @@
         count = count + there.astype(jnp.int32)
     pl.semaphore_wait(barrier, count)
 
-    part = 8 // CHUNKS
-
-    def relay(stage, way, chunk):
-        first, slots = ((right_ref, relay_b), (coef_ref, relay_k))[way]
-        rows = pl.ds(chunk * part, part)
-        source = first.at[rows] if stage == 0 else slots.at[stage - 1, rows]
+    def swap(which):
+        source, target = ((coef_ref, relay_k), (right_ref, relay_b))[which]
         return pltpu.make_async_remote_copy(
-            src_ref=source, dst_ref=slots.at[stage, rows],
-            send_sem=relay_send.at[stage, way, chunk], recv_sem=relay_recv.at[stage, way, chunk],
-            device_id=along_z(reach if way == 0 else -reach), device_id_type=MESH)
-
-    for stage in range(stages):
-        for chunk in range(CHUNKS):
-            for way in range(2):
-                if stage:
-                    relay(stage - 1, way, chunk).wait_recv()
-                relay(stage, way, chunk).start()
-    for chunk in range(CHUNKS):
-        for way in range(2):
-            relay(stages - 1, way, chunk).wait_recv()
-    for stage in range(stages):
-        for chunk in range(CHUNKS):
-            for way in range(2):
-                relay(stage, way, chunk).wait_send()
+            src_ref=source, dst_ref=target, send_sem=relay_send.at[which], recv_sem=relay_recv.at[which],
+            device_id=across, device_id_type=MESH)
+
+    swap(0).start()
+    swap(1).start()
+    swap(0).wait()
 
     row = lax.broadcasted_iota(jnp.int32, (16, 128), 0)
     lane = lax.broadcasted_iota(jnp.int32, (16, 128), 1)
@@ -395,10 +376,145 @@
         value = value + jnp.where(lax.rem(wide_lane, 4) < 2, pltpu.roll(value, 254, 1), pltpu.roll(value, 2, 1))
         return value * 0.125
 
+    tall_row, tall_lane = (lax.broadcasted_iota(jnp.int32, (32, 256), d) for d in range(2))
+    tall_odd = lax.rem(tall_lane, 2)
+    strip = lax.broadcasted_iota(jnp.int32, (32, 128), 1)
+    inner = x < half - 1
+    outer = x > 0
+
+    def side_copies(which, ref, near, far):
+        def to(index, arrival, source, target, device):
+            return pltpu.make_async_remote_copy(
+                src_ref=source, dst_ref=ref.at[target, 0:16, owned], send_sem=side_send.at[which, index],
+                recv_sem=side_recv.at[which, arrival], device_id=device, device_id_type=MESH)
+
+        low, high = slice(0, 5), slice(13, 18)
+        sent = (
+            (inner, to(0, 0, near.at[3:8], low, x_right)),
+            ((x == half - 1) & (own == 1), to(1, 0, far.at[3:8], low, x_right)),
+            (outer, to(2, 1, near.at[0:5], high, x_left)),
+            ((x == 0) & (own == 0), to(3, 1, far.at[0:5], high, x_left)),
+        )
+        arrive = ((outer | (own == 1), to(0, 0, near.at[3:8], low, x_right)),
+                  (inner | (own == 0), to(2, 1, near.at[0:5], high, x_left)))
+        return sent, arrive
+
+    def side_start(which, ref, near, far):
+        ref[5:13, 0:16, owned] = near[...]
+        each(side_copies(which, ref, near, far)[0], lambda copy: copy.start())
+
+    def side_finish(which, ref, near, far):
+        sent, arrive = side_copies(which, ref, near, far)
+        each(arrive, lambda copy: copy.wait_recv())
+        each(sent, lambda copy: copy.wait_send())
+
+    def deep_copies(which, ref):
+        def to(index, source, target, device):
+            return pltpu.make_async_remote_copy(
+                src_ref=source, dst_ref=target, send_sem=deep_send.at[which, index],
+                recv_sem=deep_recv.at[which, index], device_id=device, device_id_type=MESH)
+
+        def pack(index, side, block, device):
+            return to(index, ez.at[which, side], er.at[which, side, block], device)
+
+        sent = (
+            (has_y_up, to(0, ref.at[:, 8:16, owned], ref.at[:, 24:32, owned], y_up)),
+            (has_y_down, to(1, ref.at[:, 0:8, owned], ref.at[:, 16:24, owned], y_down)),
+            (has_z_up, pack(2, 0, 0, z_up)),
+            (has_z_down, pack(3, 1, 0, z_down)),
+            (corners[0][0], pack(4, 0, 2, corners[0][1])),
+            (corners[1][0], pack(5, 1, 2, corners[1][1])),
+            (corners[2][0], pack(6, 0, 1, corners[2][1])),
+            (corners[3][0], pack(7, 1, 1, corners[3][1])),
+        )
+        opposite = (has_y_down, has_y_up, has_z_down, has_z_up,
+                    corners[3][0], corners[2][0], corners[1][0], corners[0][0])
+        return sent, tuple((there, sent[i][1]) for i, there in enumerate(opposite))
+
+    def deep_start(which, ref):
+        high, low = jnp.zeros((16, 128), jnp.float32), jnp.zeros((16, 128), jnp.float32)
+        for i in range(18):
+            value = ref[i, 0:16, owned]
+            here = (lane >= 7 * i) & (lane < 7 * i + 7)
+            high = jnp.where(here, pltpu.roll(value, (7 * i + 7) % 128, 1), high)
+            low = jnp.where(here, pltpu.roll(value, 7 * i, 1), low)
+        ez[which, 0] = high
+        ez[which, 1] = low
+        each(deep_copies(which, ref)[0], lambda copy: copy.start())
+
+    def deep_finish(which, ref):
+        sent, arrive = deep_copies(which, ref)
+        each(arrive, lambda copy: copy.wait_recv())
+        each(sent, lambda copy: copy.wait_send())
+        below, above = (
+            jnp.concatenate([er[which, side, 0], er[which, side, 1, 0:8], er[which, side, 2, 8:16]]) for side in range(2))
+        for i in range(18):
+            ref[i, :, 128:256] = jnp.where(
+                strip < 7, pltpu.roll(above, (128 - 7 * i) % 128, 1),
+                jnp.where(strip >= 121, pltpu.roll(below, (121 - 7 * i) % 128, 1), 0.0))
+
+    def deep_around(ref, a, b):
+        value = ref[a:b]
+        return value, (
+            ref[a - 1 : b - 1], ref[a + 1 : b + 1], pltpu.roll(value, 1, 1), pltpu.roll(value, 31, 1),
+            pltpu.roll(value, 1, 2), pltpu.roll(value, 255, 2),
+        )
+
+    def deep_faces():
+        for i in range(1, 17):
+            value, around = deep_around(ek, i, i + 1)
+            faces = [0.5 * (value + other) for other in around]
+            diagonal = faces[0]
+            for face in faces[1:]:
+                diagonal = diagonal + face
+            inverse = jnp.where(value > 0.0, 1.0 / diagonal, 0.0)
+            for f in range(6):
+                eg[f, i - 1 : i] = faces[f] * inverse
+            eb[i : i + 1] = eb[i : i + 1] * inverse
+
+    def deep_total(ref, a, b):
+        value, around = deep_around(ref, a, b)
+        total = eb[a:b] - value
+        for f in range(6):
+            total = total + eg[f, a - 1 : b - 1] * around[f]
+        return value, total
+
+    def deep_correct(coarse):
+        for j in range(-3, 7):
+            spot = 4 * x + j
+            kind = own
+            place = 1 + spot
+            if j < 0:
+                wrapped = spot < 0
+                place = jnp.where(wrapped, place + count1, place)
+                kind = jnp.where(wrapped, 0, own)
+                there = jnp.logical_not(wrapped & (own == 0))
+            elif j > 3:
+                wrapped = spot >= count1
+                place = jnp.where(wrapped, place - count1, place)
+                kind = jnp.where(wrapped, 1, own)
+                there = jnp.logical_not(wrapped & (own == 1))
+            else:
+                there = None
+            value = coarse[place]
+            value = jnp.where(lax.rem(wide_lane, 2) == kind, value,
+                              jnp.where(odd, pltpu.roll(value, 1, 1), pltpu.roll(value, 255, 1)))
+            if there is not None:
+                value = jnp.where(there, value, 0.0)
+            for shift in range(2):
+                for c in range(2):
+                    cols = slice(128 * c, 128 * c + 128)
+                    spill[c, pl.ds(shift, 8, stride=2), :] = value[0:8, cols]
+                    spill[c, pl.ds(16 + shift, 4, stride=2), :] = value[8:12, cols]
+                    spill[c, pl.ds(24 + shift, 4, stride=2), :] = value[20:24, cols]
+            for i in (2 * j + 5, 2 * j + 6):
+                if 0 <= i < 18:
+                    for c in range(2):
+                        cols = slice(128 * c, 128 * c + 128)
+                        exa[i, :, cols] = exa[i, :, cols] + spill[c]
+
     xs[0][0, own, 1:9] = coef_ref[...]
-    xs[0][0, 1 - own, 1:9] = relay_k[stages - 1]
-    bs[0][own] = right_ref[...]
-    bs[0][1 - own] = relay_b[stages - 1]
+    xs[0][0, 1 - own, 1:9] = relay_k[...]
     start(0, 0)
     gather_start(0, k1, 1, [restrict(xs[0][0, s, 1:9], 1) for s in range(2)])
     finish(0, 0)
@@ -413,32 +529,49 @@
             gs[0][i, s] = faces[i] * inverse
         ds[0][0, s] = diagonal
         ds[0][1, s] = inverse
-        bs[0][s] = bs[0][s] * inverse
+    swap(1).wait()
+    bs[0][own] = right_ref[...]
+    bs[0][1 - own] = relay_b[...]
+    for s in range(2):
+        bs[0][s] = bs[0][s] * ds[0][1, s]
     state["par"] = 1
 
     def between(sweep):
         if sweep == 0:
             gather_finish(0, k1, 1)
             cross_start(0, k1, 1, count1)
+            side_start(0, ek, coef_ref, relay_k)
+            side_start(1, eb, right_ref, relay_b)
         if sweep == 1:
             cross_finish(0, k1, 1, count1)
+            side_finish(0, ek, coef_ref, relay_k)
+            side_finish(1, eb, right_ref, relay_b)
+            deep_start(0, ek)
+            deep_start(1, eb)
             coarse_faces(1, k1, count1, g1, d1)
         if sweep == 2:
             for m in range(count2):
                 k2[1 + m] = coarse_restrict(k1[1 + 2 * m : 3 + 2 * m])
             coarse_faces(2, k2, count2, g2, d2)
+            deep_finish(0, ek)
+            deep_finish(1, eb)
 
     smooth(0, True, between)
     held = state["par"]
     start(0, held)
+    near, far = xs[0].at[held, own, 1:9], xs[0].at[held, 1 - own, 1:9]
+    side_start(2, exa, near, far)
     finish(0, held)
     fine = []
     for s in range(2):
         _, total = scaled_residual(0, held, s)
         fine.append(restrict(total * ds[0][0, s], 1))
     gather_start(1, r1, 0, fine)
+    side_finish(2, exa, near, far)
+    deep_start(2, exa)
     gather_finish(1, r1, 0)
     cross_start(1, r1, 0, count1)
+    deep_faces()
     cross_finish(1, r1, 0, count1)
     for a, b in groups(count1):
         r1[a:b] = r1[a:b] * d1[1, a:b]
@@ -455,34 +588,34 @@
     for q in range(count1):
         x1s[1 + q, mine, owned] = now[1 + q, mine, owned] + deep[1 + q // 2, mine, owned]
     cross_start(3, x1s, 1, count1)
+    deep_finish(2, exa)
     cross_finish(3, x1s, 1, count1)
     now = coarse_smooth(1, x1s, [x1a, x1b], count1, r1, g1, u1)
-    par = 1 - held
-    for p in range(4):
-        value = now[1 + 4 * x + p, mine, owned]
-        for s in range(2):
-            half_of = jnp.where(odd8, value, pltpu.roll(value, 127, 1)) if s else jnp.where(odd8, pltpu.roll(value, 1, 1), value)
-            wide[s, p, pl.ds(0, 8, stride=2), :] = half_of
-            wide[s, p, pl.ds(1, 8, stride=2), :] = half_of
-    for s in range(2):
-        for p in range(8):
-            xs[0][par, s, 1 + p] = xs[0][held, s, 1 + p] + wide[s, p // 2]
-    state["par"] = par
-    smooth(0, False)
-    par = state["par"]
-    start(0, par)
-    finish(0, par)
-    for s in range(2):
-        @pl.when(own == s)
-        def _():
-            value, total = scaled_residual(0, par, s)
-            sol_ref[...] = value
-            res_ref[...] = total * ds[0][0, s]
+    deep_correct(now)
+    rho = 1.0 / SIGMA
+    sweeps = [(0.0, 1.0 / CENTRE)]
+    for _ in range(DEGREE - 1):
+        rho_next = 1.0 / (2.0 * SIGMA - rho)
+        sweeps.append((rho_next * rho, 2.0 * rho_next / HALF))
+        rho = rho_next
+    now, then = exa, exb
+    for depth, (old, new) in enumerate(sweeps):
+        for i in range(1 + depth, 17 - depth):
+            value, total = deep_total(now, i, i + 1)
+            u = new * total
+            if old:
+                u = old * eu[i - 1 : i] + u
+            eu[i - 1 : i] = u
+            then[i : i + 1] = value + u
+        now, then = then, now
+    for p in range(8):
+        value, total = deep_total(now, 5 + p, 6 + p)
+        sol_ref[p] = value[0, 0:16, owned]
+        res_ref[p] = total[0, 0:16, owned] * ds[0][0, own, p]
 
 
 def solution(mesh):
     sizes = tuple(mesh.shape[a] for a in ("gx", "gy", "gz"))
-    stages = 4 if sizes[1] % 4 == 0 else sizes[1]
     vmem = pltpu.VMEM
     f32 = jnp.float32
     half = sizes[0] // 2
@@ -496,12 +629,15 @@
         vmem((2, 2, 10, 16, 128), f32), vmem((6, 2, 8, 16, 128), f32), vmem((2, 8, 16, 128), f32),
         vmem((2, 8, 16, 128), f32), vmem((2, 2, 8, 16, 128), f32),
         *[vmem((1, 2, 2, 16, 128), f32)] * 4,
-        *[vmem((stages, 8, 16, 128), f32)] * 2,
-        *[dma((1, 2, 8))] * 2, *[dma((stages, 2, CHUNKS))] * 2,
+        *[vmem((8, 16, 128), f32)] * 2,
+        *[dma((1, 2, 8))] * 2, *[dma((2,))] * 2,
         big(n1 + 2), big(n1), big(n1 + 2), big(n1 + 2), big(n1 + 2), big(6, n1), big(n1), big(2, n1),
         big(n2 + 2), big(n2), big(n2 + 2), big(n2 + 2), big(6, n2), big(n2), big(2, n2),
         vmem((2, 4, 16, 128), f32), vmem((4, 2, 2, 8, 128), f32), vmem((4, 2, 3, 2, 8, 128), f32),
         *[dma((2, half))] * 2, *[dma((4, 8))] * 2,
+        *[vmem((18, 32, 256), f32)] * 4, vmem((6, 16, 32, 256), f32), vmem((16, 32, 256), f32),
+        vmem((3, 2, 16, 128), f32), vmem((3, 2, 3, 16, 128), f32), *[dma((3, 4))] * 2, *[dma((3, 8))] * 2,
+        vmem((2, 32, 128), f32),
     ]
 
     def per_device(right_side, coefficient):

time: 115 us -> 99.8 us (0.87)
  Pallas kernels: 112 us -> 96.8 us
    pallas_call x1, Pallas kernels: 112 us -> 96.8 us  [per_device(): pl.pallas_call(functools.partial(kernel, sizes), out_shape=(jax.ShapeDtyp...]
where the time goes in v3:
time: 99.8 us; the launch traced here: 99.5 us
  Pallas kernels  96.8 us (97%)
  local copies, waits for them, and re-layouts  2.14 us (2%)
    pallas_call x1, Pallas kernels, per_device(): pl.pallas_call(functools.partial(kernel, sizes), out_shape=(jax.ShapeDtyp...  96.8 us
    unnamed x4, local copies, waits for them, and re-layouts  2.14 us

profile of v3, /device:TPU:1, one launch (start us, length us, event | category | flops | bytes accessed | tf_op | source)
XLA Modules:
  0.0 99.5 jit_solution(2494399607802740633)
XLA Ops:
  0.6 96.8 %vcycle.1 = (f32[8,16,128]{2,1,0:T(8,128)}, f32[8,16,128]{2,1,0:T(8,128)}) custom-call(f32[8,16,128]{2,1,0:T(8,128)} %right_ref.1, f32[8,16,128]{2,1,0:T(8,128)} %coef_ref.1), custom_call_target="tpu_custom_call" | custom-call | tf_op jit(solution)/shard_map/vcycle/pallas_call | solution.py:644
  97.4 0.0 copy-start
  97.4 1.5 %copy.6 = f32[8,16,128]{2,1,0:T(8,128)} copy(f32[8,16,128]{2,1,0:T(8,128)} %get-tuple-element.4) | data formatting | bytes 131072
  98.9 0.0 copy-done
  98.9 0.6 copy.7
Async XLA Ops:
  97.4 1.5 %copy-start = (f32[8,16,128]{2,1,0:T(8,128)S(1)}, f32[8,16,128]{2,1,0:T(8,128)}, u32[]{:S(2)}) copy-start(f32[8,16,128]{2,1,0:T(8,128)} %get-tuple-element.5) | copy-start | bytes 196612

commit v4 on v3

--- a/solution.py
+++ b/solution.py
@@ -72,8 +72,9 @@
             device_id=across, device_id_type=MESH)
 
     swap(0).start()
+    swap(0).wait_send()
     swap(1).start()
-    swap(0).wait()
+    swap(0).wait_recv()
 
     row = lax.broadcasted_iota(jnp.int32, (16, 128), 0)
     lane = lax.broadcasted_iota(jnp.int32, (16, 128), 1)
@@ -546,15 +547,11 @@
             cross_finish(0, k1, 1, count1)
             side_finish(0, ek, coef_ref, relay_k)
             side_finish(1, eb, right_ref, relay_b)
-            deep_start(0, ek)
-            deep_start(1, eb)
             coarse_faces(1, k1, count1, g1, d1)
         if sweep == 2:
             for m in range(count2):
                 k2[1 + m] = coarse_restrict(k1[1 + 2 * m : 3 + 2 * m])
             coarse_faces(2, k2, count2, g2, d2)
-            deep_finish(0, ek)
-            deep_finish(1, eb)
 
     smooth(0, True, between)
     held = state["par"]
@@ -571,7 +568,6 @@
     deep_start(2, exa)
     gather_finish(1, r1, 0)
     cross_start(1, r1, 0, count1)
-    deep_faces()
     cross_finish(1, r1, 0, count1)
     for a, b in groups(count1):
         r1[a:b] = r1[a:b] * d1[1, a:b]
@@ -581,6 +577,8 @@
         _, total = coarse_total(1, now, 2 * m, 2 * m + 2, r1, g1)
         r2[m, mine, owned] = coarse_restrict(total * d1[0, 2 * m : 2 * m + 2])[mine, owned]
     cross_start(2, r2, 0, count2)
+    deep_start(0, ek)
+    deep_start(1, eb)
     cross_finish(2, r2, 0, count2)
     for a, b in groups(count2):
         r2[a:b] = r2[a:b] * d2[1, a:b]
@@ -589,6 +587,9 @@
         x1s[1 + q, mine, owned] = now[1 + q, mine, owned] + deep[1 + q // 2, mine, owned]
     cross_start(3, x1s, 1, count1)
     deep_finish(2, exa)
+    deep_finish(0, ek)
+    deep_finish(1, eb)
+    deep_faces()
     cross_finish(3, x1s, 1, count1)
     now = coarse_smooth(1, x1s, [x1a, x1b], count1, r1, g1, u1)
     deep_correct(now)
@@ -641,7 +642,7 @@
     ]
 
     def per_device(right_side, coefficient):
-        return pl.pallas_call(
+        found = pl.pallas_call(
             functools.partial(kernel, sizes),
             out_shape=(jax.ShapeDtypeStruct((8, 16, 128), f32),) * 2,
             in_specs=[pl.BlockSpec(memory_space=vmem)] * 2,
@@ -651,5 +652,17 @@
             name="vcycle",
         )(right_side, coefficient)
 
+        def hand_on(a_ref, b_ref, c_ref, d_ref):
+            c_ref[...] = a_ref[...]
+            d_ref[...] = b_ref[...]
+
+        return pl.pallas_call(
+            hand_on,
+            out_shape=(jax.ShapeDtypeStruct((8, 16, 128), f32),) * 2,
+            in_specs=[pl.BlockSpec(memory_space=vmem)] * 2,
+            out_specs=(pl.BlockSpec(memory_space=vmem),) * 2,
+            name="hand_on",
+        )(*found)
+
     specs = (P("gx", "gy", "gz"), P("gx", "gy", "gz"))
     return jax.shard_map(per_device, mesh=mesh, in_specs=specs, out_specs=specs, check_vma=False)

time: 99.8 us -> 97.5 us (0.977)
  local copies, waits for them, and re-layouts: 2.14 us -> 0 us
    unnamed x4 -> x0, local copies, waits for them, and re-layouts: 2.14 us -> none
    pallas_call x1, Pallas kernels: 96.8 us -> 95.1 us  [per_device(): pl.pallas_call(functools.partial(kernel, sizes), out_shape=(jax.ShapeDtyp...]
    pallas_call x0 -> x1, Pallas kernels: none -> 1.53 us  [per_device(): pl.pallas_call(hand_on, out_shape=(jax.ShapeDtypeStruct((8, 16, 128), f32...]
where the time goes in v4:
time: 97.5 us; the launch traced here: 97.2 us
  Pallas kernels  96.6 us (99%)
    pallas_call x1, Pallas kernels, per_device(): pl.pallas_call(functools.partial(kernel, sizes), out_shape=(jax.ShapeDtyp...  95.1 us

profile of v4, /device:TPU:1, one launch (start us, length us, event | category | flops | bytes accessed | tf_op | source)
XLA Modules:
  0.0 97.2 jit_solution(3860640971772966976)
XLA Ops:
  0.6 95.1 %vcycle.1 = (f32[8,16,128]{2,1,0:T(8,128)}, f32[8,16,128]{2,1,0:T(8,128)}) custom-call(f32[8,16,128]{2,1,0:T(8,128)} %right_ref.1, f32[8,16,128]{2,1,0:T(8,128)} %coef_ref.1), custom_call_target="tpu_custom_call" | custom-call | tf_op jit(solution)/shard_map/vcycle/pallas_call | solution.py:645
  95.7 1.5 %hand_on.1 = (f32[8,16,128]{2,1,0:T(8,128)}, f32[8,16,128]{2,1,0:T(8,128)}) custom-call(f32[8,16,128]{2,1,0:T(8,128)} %get-tuple-element.4.a_ref, f32[8,16,128]{2,1,0:T(8,128)} %get-tuple-element.5.b_ref), custom_call_target="tpu_custom_call" | custom-call | tf_op jit(solution)/shard_map/hand_on/pallas_call | solution.py:659
